TPU v7x, 512 devices: a whole 4x4x16 slice. The times are simulated.
512 devices in a mesh: seg: 512 (over z, x, y, core).
Axes of the slice: x: 4, y: 4, z: 16, core: 2. Of those that a mesh axis runs over, the one named last changes fastest.
Arguments:
- density: float32 [2, 196608, 256], P(None, 'seg'), may hold values from -6 to 6
- near_blocks: bfloat16 [3, 2, 196608, 384], P(None, None, 'seg'), may hold values from -0.21875 to 0.21875
- projection: bfloat16 [2, 98304, 384], P(None, 'seg'), may hold values from -0.21875 to 0.21875
- transfers: bfloat16 [5, 2, 98304, 192], P(None, None, 'seg'), may hold values from -0.3125 to 0.3125
- interpolation: bfloat16 [2, 196608, 192], P(None, 'seg'), may hold values from -0.3125 to 0.3125
- precondition: float32 [2, 196608], P(None, 'seg'), may hold values from 0.5 to 1.5
Outputs:
- result: float32 [2, 196608, 256], P(None, 'seg')
All inputs are finite; a program needn't handle non-finite values.
Results may differ from a plain program's by a relative error of at most 0.007.
Values may be sent and summed in bfloat16 or wider, within the bound.
No kernel may reach another device: no remote copies, remote signals or barrier semaphores. Data moves between devices by JAX's collectives and lax.ppermute only.
A program may use at most 64 MiB of HBM per device.

v0:
```python
import jax
import jax.numpy as jnp
from jax import lax
from jax.sharding import PartitionSpec as P


def passed_along(block, axis, distance):
    devices = range(lax.axis_size(axis))
    route = [((i - distance) % len(devices), i) for i in devices]
    return lax.ppermute(block, axis, route)


def swapped(array, axis, apart):
    return lax.ppermute(array, axis, [(i, i ^ 1 << apart) for i in range(lax.axis_size(axis))])


def matmul_f32(left, right):
    return jnp.dot(left, right, preferred_element_type=jnp.float32)


def complex_product(matrix, vector):
    real_part = matmul_f32(matrix[0], vector[0]) - matmul_f32(matrix[1], vector[1])
    imag_part = matmul_f32(matrix[0], vector[1]) + matmul_f32(matrix[1], vector[0])
    return jnp.stack([real_part, imag_part])


def body(density, near_blocks, projection, transfers, interpolation, precondition):
    own_rows = density.astype(jnp.bfloat16)
    before = passed_along(own_rows, "seg", 1)
    after = passed_along(own_rows, "seg", -1)
    coeffs = complex_product(projection, own_rows)
    near = complex_product(near_blocks[0], own_rows)
    near = near + complex_product(near_blocks[1], before)
    near = near + complex_product(near_blocks[2], after)
    position = lax.axis_index("seg")
    half_rows = projection.shape[1] // 2
    for level_no in range(transfers.shape[0]):
        rounded = coeffs.astype(jnp.bfloat16)
        lower_half = jnp.bitwise_and(jnp.right_shift(position, level_no), 1) == 0
        other_block = swapped(rounded, "seg", level_no)
        joined = jnp.where(
            lower_half,
            jnp.concatenate([rounded[:, :half_rows], other_block[:, :half_rows]], axis=1),
            jnp.concatenate([other_block[:, half_rows:], rounded[:, half_rows:]], axis=1),
        )
        coeffs = complex_product(transfers[level_no], joined)
    far = complex_product(interpolation, coeffs.astype(jnp.bfloat16))
    total = near + far
    pre_real = precondition[0][:, None]
    pre_imag = precondition[1][:, None]
    return jnp.stack(
        [pre_real * total[0] - pre_imag * total[1], pre_real * total[1] + pre_imag * total[0]]
    )


def solution(mesh):
    placed = (
        P(None, "seg", None),
        P(None, None, "seg", None),
        P(None, "seg", None),
        P(None, None, "seg", None),
        P(None, "seg", None),
        P(None, "seg"),
    )
    return jax.shard_map(
        body, mesh=mesh, in_specs=placed, out_specs=P(None, "seg", None), check_vma=False
    )
```

profile of v0, /device:TPU:8, one launch (start us, length us, event | category | flops | bytes accessed | tf_op | source)
XLA Modules:
  0.0 71.5 jit_solution(15437726909981071532)
XLA Ops:
  0.0 1.3 %convert_element_type.2 = bf16[2,384,256]{2,1,0:T(8,128)(2,1)S(1)} convert(f32[2,384,256]{2,1,0:T(8,128)} %param.6) | non-fusion elementwise | flops 196608 | bytes 1179648 | tf_op jit(solution)/shard_map/convert_element_type | solution.py:28
  1.3 1.9 %collective-permute-start.1 = (bf16[2,384,256]{2,1,0:T(8,128)(2,1)S(1)}, bf16[2,384,256]{2,1,0:T(8,128)(2,1)}, u32[]{:S(2)}, u32[]{:S(2)}) collective-permute-start(bf16[2,384,256]{2,1,0:T(8,128)(2,1)S(1)} %convert_element_type.2), channel_id=1, source_target_pairs={{1,0},{2,1},{3,2},{4,3},{5,4},{6,5},{7,6},{8,7},{9,8},{10,9},{11,1... | collective-permute-start | bytes 1179656 | tf_op jit(solution)/shard_map/ppermute | solution.py:10
  3.3 2.4 %collective-permute-start = (bf16[2,384,256]{2,1,0:T(8,128)(2,1)S(1)}, bf16[2,384,256]{2,1,0:T(8,128)(2,1)S(1)}, u32[]{:S(2)}, u32[]{:S(2)}) collective-permute-start(bf16[2,384,256]{2,1,0:T(8,128)(2,1)S(1)} %convert_element_type.2), channel_id=1, source_target_pairs={{511,0},{0,1},{1,2},{2,3},{3,4},{4,5},{5,6},{6,7},{7,8},{8,9},{9,1... | collective-permute-start | bytes 1179656 | tf_op jit(solution)/shard_map/ppermute | solution.py:10
  5.7 1.1 %fusion.70 = f32[192,256]{1,0:T(8,128)S(1)} fusion(bf16[2,192,384]{2,1,0:T(8,128)(2,1)} %param.8, bf16[2,384,256]{2,1,0:T(8,128)(2,1)S(1)} %convert_element_type.2), kind=kOutput, calls=%fused_computation.130 | convolution fusion | flops 37748736 | bytes 540672 | tf_op jit(solution)/shard_map/dot_general | solution.py:18
  8.1 3.1 %collective-permute-start.2 = (bf16[2,192,256]{2,1,0:T(8,128)(2,1)}, bf16[2,192,256]{2,1,0:T(8,128)(2,1)}, u32[]{:S(2)}, u32[]{:S(2)}) collective-permute-start(bf16[2,192,256]{2,1,0:T(8,128)(2,1)} %pad_maximum_fusion.1), channel_id=1, source_target_pairs={{0,1},{1,0},{2,3},{3,2},{4,5},{5,4},{6,7},{7,6},{8,9},{9,8},{10,11... | collective-permute-start | bytes 589832 | tf_op jit(solution)/shard_map/ppermute | solution.py:14
  11.5 1.0 %fusion.46 = f32[384,256]{1,0:T(8,128)} fusion(bf16[3,2,384,384]{3,2,1,0:T(8,128)(2,1)S(1)} %copy-done, bf16[2,384,256]{2,1,0:T(8,128)(2,1)S(1)} %convert_element_type.2), kind=kOutput, calls=%fused_computation.70 | convolution fusion | flops 75497472 | bytes 884736 | tf_op jit(solution)/shard_map/dot_general | solution.py:18
  12.5 1.0 %fusion.7 = f32[1,384,256]{2,1,0:T(8,128)} fusion(f32[384,256]{1,0:T(8,128)S(1)} %fusion.48, bf16[3,2,384,384]{3,2,1,0:T(8,128)(2,1)S(1)} %copy-done, bf16[2,384,256]{2,1,0:T(8,128)(2,1)S(1)} %convert_element_type.2), kind=kOutput, calls=%fused_computation.15 | convolution fusion | flops 75595776 | bytes 1277952 | tf_op jit(solution)/shard_map/dot_general | solution.py:18
  14.2 1.2 %fusion.6 = f32[1,384,256]{2,1,0:T(8,128)S(1)} fusion(f32[384,256]{1,0:T(8,128)} %fusion.46, bf16[3,2,384,384]{3,2,1,0:T(8,128)(2,1)S(1)} %copy-done, bf16[2,384,256]{2,1,0:T(8,128)(2,1)S(1)} %convert_element_type.2), kind=kOutput, calls=%fused_computation.13 | convolution fusion | flops 75595776 | bytes 1277952 | tf_op jit(solution)/shard_map/dot_general | solution.py:18
  15.5 1.0 %fusion.146 = (bf16[2,96,256]{2,1,0:T(8,128)(2,1)S(1)}, bf16[2,96,256]{2,1,0:T(8,128)(2,1)S(1)}) fusion(bf16[2,192,256]{2,1,0:T(8,128)(2,1)} %collective-permute-done.2), kind=kLoop, calls=%fused_computation.218 | loop fusion | bytes 393216 | tf_op jit(solution)/shard_map/slice | solution.py:44
  16.4 1.0 %maximum_select_fusion = bf16[2,192,256]{2,1,0:T(8,128)(2,1)S(1)} fusion(bf16[2,96,256]{2,1,0:T(8,128)(2,1)S(1)} %get-tuple-element.26, bf16[2,96,256]{2,1,0:T(8,128)(2,1)} %get-tuple-element.28, bf16[2,96,256]{2,1,0:T(8,128)(2,1)} %get-tuple-element.27, bf16[2,96,256]{2,1,0:T(8,128)(2,1)S(1)} %get-tuple-element.25, pred[]{:T(512)S(6)} %eq.19), kind=kLoop, calls=%fused_computation.117 | loop fusion | flops 884736 | bytes 589825 | tf_op jit(solution)/shard_map/jit(_where)/select_n | solution.py:41
  18.2 14.3 %collective-permute-start.3 = (bf16[2,192,256]{2,1,0:T(8,128)(2,1)S(1)}, bf16[2,192,256]{2,1,0:T(8,128)(2,1)S(1)}, u32[]{:S(2)}, u32[]{:S(2)}) collective-permute-start(bf16[2,192,256]{2,1,0:T(8,128)(2,1)S(1)} %pad_maximum_fusion.2), channel_id=1, source_target_pairs={{0,2},{1,3},{2,0},{3,1},{4,6},{5,7},{6,4},{7,5},{8,10},{9,11},{10,... | collective-permute-start | bytes 589832 | tf_op jit(solution)/shard_map/ppermute | solution.py:14
  32.5 5.5 %collective-permute-done.3 = bf16[2,192,256]{2,1,0:T(8,128)(2,1)S(1)} collective-permute-done((bf16[2,192,256]{2,1,0:T(8,128)(2,1)S(1)}, bf16[2,192,256]{2,1,0:T(8,128)(2,1)S(1)}, u32[]{:S(2)}, u32[]{:S(2)}) %collective-permute-start.3) | collective-permute-done | bytes 196640 | tf_op jit(solution)/shard_map/ppermute | solution.py:14
  38.8 1.9 %collective-permute-start.4 = (bf16[2,192,256]{2,1,0:T(8,128)(2,1)S(1)}, bf16[2,192,256]{2,1,0:T(8,128)(2,1)S(1)}, u32[]{:S(2)}, u32[]{:S(2)}) collective-permute-start(bf16[2,192,256]{2,1,0:T(8,128)(2,1)S(1)} %pad_maximum_fusion.3), channel_id=1, source_target_pairs={{0,4},{1,5},{2,6},{3,7},{4,0},{5,1},{6,2},{7,3},{8,12},{9,13},{10,... | collective-permute-start | bytes 589832 | tf_op jit(solution)/shard_map/ppermute | solution.py:14
  40.8 1.2 %fusion.32 = f32[384,256]{1,0:T(8,128)S(1)} fusion(bf16[3,2,384,384]{3,2,1,0:T(8,128)(2,1)S(1)} %copy-done, bf16[2,384,256]{2,1,0:T(8,128)(2,1)} %collective-permute-done.1), kind=kOutput, calls=%fused_computation.56 | convolution fusion | flops 75497472 | bytes 884736 | tf_op jit(solution)/shard_map/dot_general | solution.py:18
  42.0 1.2 %fusion.34 = f32[384,256]{1,0:T(8,128)S(1)} fusion(bf16[3,2,384,384]{3,2,1,0:T(8,128)(2,1)S(1)} %copy-done, bf16[2,384,256]{2,1,0:T(8,128)(2,1)} %collective-permute-done.1), kind=kOutput, calls=%fused_computation.58 | convolution fusion | flops 75497472 | bytes 884736 | tf_op jit(solution)/shard_map/dot_general | solution.py:18
  43.7 1.2 %fusion.2 = f32[1,384,256]{2,1,0:T(8,128)S(1)} fusion(f32[384,256]{1,0:T(8,128)S(1)} %fusion.32, bf16[3,2,384,384]{3,2,1,0:T(8,128)(2,1)S(1)} %copy-done, bf16[2,384,256]{2,1,0:T(8,128)(2,1)} %collective-permute-done.1), kind=kOutput, calls=%fused_computation.5 | convolution fusion | flops 75595776 | bytes 1277952 | tf_op jit(solution)/shard_map/dot_general | solution.py:18
  44.9 1.2 %fusion.3 = f32[1,384,256]{2,1,0:T(8,128)S(1)} fusion(f32[384,256]{1,0:T(8,128)S(1)} %fusion.34, bf16[3,2,384,384]{3,2,1,0:T(8,128)(2,1)S(1)} %copy-done, bf16[2,384,256]{2,1,0:T(8,128)(2,1)} %collective-permute-done.1), kind=kOutput, calls=%fused_computation.7 | convolution fusion | flops 75595776 | bytes 1277952 | tf_op jit(solution)/shard_map/dot_general | solution.py:18
  46.1 2.9 %collective-permute-done.4 = bf16[2,192,256]{2,1,0:T(8,128)(2,1)S(1)} collective-permute-done((bf16[2,192,256]{2,1,0:T(8,128)(2,1)S(1)}, bf16[2,192,256]{2,1,0:T(8,128)(2,1)S(1)}, u32[]{:S(2)}, u32[]{:S(2)}) %collective-permute-start.4) | collective-permute-done | bytes 196640 | tf_op jit(solution)/shard_map/ppermute | solution.py:14
  49.8 1.9 %collective-permute-start.5 = (bf16[2,192,256]{2,1,0:T(8,128)(2,1)S(1)}, bf16[2,192,256]{2,1,0:T(8,128)(2,1)S(1)}, u32[]{:S(2)}, u32[]{:S(2)}) collective-permute-start(bf16[2,192,256]{2,1,0:T(8,128)(2,1)S(1)} %pad_maximum_fusion.4), channel_id=1, source_target_pairs={{0,8},{1,9},{2,10},{3,11},{4,12},{5,13},{6,14},{7,15},{8,0},{9,1},... | collective-permute-start | bytes 589832 | tf_op jit(solution)/shard_map/ppermute | solution.py:14
  52.0 5.5 %collective-permute-done.5 = bf16[2,192,256]{2,1,0:T(8,128)(2,1)S(1)} collective-permute-done((bf16[2,192,256]{2,1,0:T(8,128)(2,1)S(1)}, bf16[2,192,256]{2,1,0:T(8,128)(2,1)S(1)}, u32[]{:S(2)}, u32[]{:S(2)}) %collective-permute-start.5) | collective-permute-done | bytes 196640 | tf_op jit(solution)/shard_map/ppermute | solution.py:14
  58.3 1.9 %collective-permute-start.6 = (bf16[2,192,256]{2,1,0:T(8,128)(2,1)S(1)}, bf16[2,192,256]{2,1,0:T(8,128)(2,1)S(1)}, u32[]{:S(2)}, u32[]{:S(2)}) collective-permute-start(bf16[2,192,256]{2,1,0:T(8,128)(2,1)S(1)} %pad_maximum_fusion.5), channel_id=1, source_target_pairs={{0,16},{1,17},{2,18},{3,19},{4,20},{5,21},{6,22},{7,23},{8,24},{9,... | collective-permute-start | bytes 589832 | tf_op jit(solution)/shard_map/ppermute | solution.py:14
  60.6 6.8 %collective-permute-done.6 = bf16[2,192,256]{2,1,0:T(8,128)(2,1)S(1)} collective-permute-done((bf16[2,192,256]{2,1,0:T(8,128)(2,1)S(1)}, bf16[2,192,256]{2,1,0:T(8,128)(2,1)S(1)}, u32[]{:S(2)}, u32[]{:S(2)}) %collective-permute-start.6) | collective-permute-done | bytes 196640 | tf_op jit(solution)/shard_map/ppermute | solution.py:14
  69.5 0.9 %copy-done.6 = f32[2,384,256]{2,1,0:T(8,128)S(1)} copy-done((f32[2,384,256]{2,1,0:T(8,128)S(1)}, f32[2,384,256]{2,1,0:T(8,128)}, u32[]{:S(2)}) %copy-start.6) | copy-done | bytes 786456
  70.6 0.9 %copy-done.7 = f32[2,384,256]{2,1,0:T(8,128)} copy-done((f32[2,384,256]{2,1,0:T(8,128)}, f32[2,384,256]{2,1,0:T(8,128)S(1)}, u32[]{:S(2)}) %copy-start.7) | copy-done | bytes 786456
  (71 shorter events, 8.7 us)
Async XLA Ops:
  0.0 6.8 %copy-start.3 = (bf16[2,192,384]{2,1,0:T(8,128)(2,1)S(1)}, bf16[2,192,384]{2,1,0:T(8,128)(2,1)}, u32[]{:S(2)}) copy-start(bf16[2,192,384]{2,1,0:T(8,128)(2,1)} %param.8) | copy-start | bytes 884740
  0.0 11.2 %copy-start = (bf16[3,2,384,384]{3,2,1,0:T(8,128)(2,1)S(1)}, bf16[3,2,384,384]{3,2,1,0:T(8,128)(2,1)}, u32[]{:S(2)}) copy-start(bf16[3,2,384,384]{3,2,1,0:T(8,128)(2,1)} %param.7) | copy-start | bytes 5308420
  1.3 39.4 %collective-permute-start.1 = (bf16[2,384,256]{2,1,0:T(8,128)(2,1)S(1)}, bf16[2,384,256]{2,1,0:T(8,128)(2,1)}, u32[]{:S(2)}, u32[]{:S(2)}) collective-permute-start(bf16[2,384,256]{2,1,0:T(8,128)(2,1)S(1)} %convert_element_type.2), channel_id=1, source_target_pairs={{1,0},{2,1},{3,2},{4,3},{5,4},{6,5},{7,6},{8,7},{9,8},{10,9},{11,1... | collective-permute-start | bytes 1179656 | tf_op jit(solution)/shard_map/ppermute | solution.py:10
  3.3 39.9 %collective-permute-start = (bf16[2,384,256]{2,1,0:T(8,128)(2,1)S(1)}, bf16[2,384,256]{2,1,0:T(8,128)(2,1)S(1)}, u32[]{:S(2)}, u32[]{:S(2)}) collective-permute-start(bf16[2,384,256]{2,1,0:T(8,128)(2,1)S(1)} %convert_element_type.2), channel_id=1, source_target_pairs={{511,0},{0,1},{1,2},{2,3},{3,4},{4,5},{5,6},{6,7},{7,8},{8,9},{9,1... | collective-permute-start | bytes 1179656 | tf_op jit(solution)/shard_map/ppermute | solution.py:10
  8.1 7.3 %collective-permute-start.2 = (bf16[2,192,256]{2,1,0:T(8,128)(2,1)}, bf16[2,192,256]{2,1,0:T(8,128)(2,1)}, u32[]{:S(2)}, u32[]{:S(2)}) collective-permute-start(bf16[2,192,256]{2,1,0:T(8,128)(2,1)} %pad_maximum_fusion.1), channel_id=1, source_target_pairs={{0,1},{1,0},{2,3},{3,2},{4,5},{5,4},{6,7},{7,6},{8,9},{9,8},{10,11... | collective-permute-start | bytes 589832 | tf_op jit(solution)/shard_map/ppermute | solution.py:14
  12.5 4.9 %copy-start.1 = (bf16[5,2,192,192]{3,2,1,0:T(8,128)(2,1)S(1)}, bf16[5,2,192,192]{3,2,1,0:T(8,128)(2,1)}, u32[]{:S(2)}) copy-start(bf16[5,2,192,192]{3,2,1,0:T(8,128)(2,1)} %param.9) | copy-start | bytes 2211844
  15.5 17.0 %copy-start.5 = (f32[2,384]{1,0:T(2,128)S(1)}, f32[2,384]{1,0:T(2,128)}, u32[]{:S(2)}) copy-start(f32[2,384]{1,0:T(2,128)} %param.11) | copy-start | bytes 9220
  18.2 19.8 %collective-permute-start.3 = (bf16[2,192,256]{2,1,0:T(8,128)(2,1)S(1)}, bf16[2,192,256]{2,1,0:T(8,128)(2,1)S(1)}, u32[]{:S(2)}, u32[]{:S(2)}) collective-permute-start(bf16[2,192,256]{2,1,0:T(8,128)(2,1)S(1)} %pad_maximum_fusion.2), channel_id=1, source_target_pairs={{0,2},{1,3},{2,0},{3,1},{4,6},{5,7},{6,4},{7,5},{8,10},{9,11},{10,... | collective-permute-start | bytes 589832 | tf_op jit(solution)/shard_map/ppermute | solution.py:14
  38.8 10.1 %collective-permute-start.4 = (bf16[2,192,256]{2,1,0:T(8,128)(2,1)S(1)}, bf16[2,192,256]{2,1,0:T(8,128)(2,1)S(1)}, u32[]{:S(2)}, u32[]{:S(2)}) collective-permute-start(bf16[2,192,256]{2,1,0:T(8,128)(2,1)S(1)} %pad_maximum_fusion.3), channel_id=1, source_target_pairs={{0,4},{1,5},{2,6},{3,7},{4,0},{5,1},{6,2},{7,3},{8,12},{9,13},{10,... | collective-permute-start | bytes 589832 | tf_op jit(solution)/shard_map/ppermute | solution.py:14
  49.8 7.8 %collective-permute-start.5 = (bf16[2,192,256]{2,1,0:T(8,128)(2,1)S(1)}, bf16[2,192,256]{2,1,0:T(8,128)(2,1)S(1)}, u32[]{:S(2)}, u32[]{:S(2)}) collective-permute-start(bf16[2,192,256]{2,1,0:T(8,128)(2,1)S(1)} %pad_maximum_fusion.4), channel_id=1, source_target_pairs={{0,8},{1,9},{2,10},{3,11},{4,12},{5,13},{6,14},{7,15},{8,0},{9,1},... | collective-permute-start | bytes 589832 | tf_op jit(solution)/shard_map/ppermute | solution.py:14
  58.3 9.1 %collective-permute-start.6 = (bf16[2,192,256]{2,1,0:T(8,128)(2,1)S(1)}, bf16[2,192,256]{2,1,0:T(8,128)(2,1)S(1)}, u32[]{:S(2)}, u32[]{:S(2)}) collective-permute-start(bf16[2,192,256]{2,1,0:T(8,128)(2,1)S(1)} %pad_maximum_fusion.5), channel_id=1, source_target_pairs={{0,16},{1,17},{2,18},{3,19},{4,20},{5,21},{6,22},{7,23},{8,24},{9,... | collective-permute-start | bytes 589832 | tf_op jit(solution)/shard_map/ppermute | solution.py:14
  60.5 7.7 %copy-start.4 = (bf16[2,384,192]{1,2,0:T(8,128)(2,1)S(1)}, bf16[2,384,192]{1,2,0:T(8,128)(2,1)}, u32[]{:S(2)}) copy-start(bf16[2,384,192]{1,2,0:T(8,128)(2,1)} %param.10) | copy-start | bytes 884740
  68.2 1.1 %copy-start.2 = (f32[1,384,256]{2,1,0:T(8,128)S(1)}, f32[1,384,256]{2,1,0:T(8,128)}, u32[]{:S(2)}) copy-start(f32[1,384,256]{2,1,0:T(8,128)} %fusion.7) | copy-start | bytes 1179652
  69.3 1.1 %copy-start.6 = (f32[2,384,256]{2,1,0:T(8,128)S(1)}, f32[2,384,256]{2,1,0:T(8,128)}, u32[]{:S(2)}) copy-start(f32[2,384,256]{2,1,0:T(8,128)} %custom-call) | copy-start | bytes 2359300
  70.6 0.9 %copy-start.7 = (f32[2,384,256]{2,1,0:T(8,128)}, f32[2,384,256]{2,1,0:T(8,128)S(1)}, u32[]{:S(2)}) copy-start(f32[2,384,256]{2,1,0:T(8,128)S(1)} %get-tuple-element.41) | copy-start | bytes 2359300
where the time goes:
time: 72 us; the launch traced here: 71.5 us
  starting transfers between devices  27.4 us (38%)
  waiting for transfers between devices  20.8 us (29%)
  matrix products  15.5 us (22%)
  other arithmetic  4.45 us (6%)
  local copies, waits for them, and re-layouts  2.86 us (4%)
    ppermute x5, starting transfers between devices, swapped(): lax.ppermute(array, axis, [(i, i ^ 1 << apart) for i in range(lax.axis_si...  23.1 us
    ppermute x5, waiting for transfers between devices, swapped(): lax.ppermute(array, axis, [(i, i ^ 1 << apart) for i in range(lax.axis_si...  20.8 us
    dot_general x40, matrix products, matmul_f32(): return jnp.dot(left, right, preferred_element_type=jnp.float32)  15.5 us
    ppermute x2, starting transfers between devices, passed_along(): return lax.ppermute(block, axis, route)  4.33 us
    unnamed x16, local copies, waits for them, and re-layouts  1.82 us
    another operation x10, other arithmetic, complex_product(): return jnp.stack([real_part, imag_part])  1.54 us
  transfers between devices with their start and end apart: 7, of which 4 were waited for; matrix products, arithmetic and copies ran while one was open for 22% of the time, Pallas kernels for 0%

commit v1 on v0

v1 whole, which is shorter than its diff:
```python
import jax
import jax.numpy as jnp
from jax import lax
from jax.experimental import pallas as pl
from jax.experimental.pallas import tpu as pltpu
from jax.sharding import PartitionSpec as P

VMEM = pl.BlockSpec(memory_space=pltpu.VMEM)
HBM = pl.BlockSpec(memory_space=pltpu.HBM)
F32 = jnp.float32
BF16 = jnp.bfloat16


def swapped(array, mask):
    return lax.ppermute(array, "seg", [(i, i ^ mask) for i in range(lax.axis_size("seg"))])


def swapped_across(array):
    size = lax.axis_size("seg")
    return lax.ppermute(array, "seg", [(i, (((i + 1) ^ 1) - 1) % size) for i in range(size)])


def held(array):
    return pltpu.with_memory_space_constraint(array, pltpu.VMEM)


def in_hbm(array):
    return pltpu.with_memory_space_constraint(array, pltpu.HBM)


def call(kernel, name, limit, out_shape, operands, in_specs=None, out_specs=None, scratch=()):
    return pl.pallas_call(
        kernel,
        out_shape=out_shape,
        in_specs=in_specs or [VMEM] * len(operands),
        out_specs=out_specs or jax.tree.map(lambda _: VMEM, out_shape),
        scratch_shapes=scratch,
        compiler_params=pltpu.CompilerParams(vmem_limit_bytes=limit << 20),
        name=name,
    )(*((in_hbm if in_specs else held)(a) for a in operands))


def dot(left, right):
    return jnp.dot(left, right, preferred_element_type=F32)


def bit_of(level):
    return jnp.bitwise_and(jnp.right_shift(lax.axis_index("seg"), level), 1)


def product(real, imag, vec_real, vec_imag):
    return (
        dot(real, vec_real) - dot(imag, vec_imag),
        dot(real, vec_imag) + dot(imag, vec_real),
    )


def store_halves(level, half, matrix, vec_real, vec_imag, keep, send):
    bit = bit_of(level)
    for target, which in ((send, 1 - bit), (keep, bit)):
        rows = pl.ds(pl.multiple_of(which * half, half), half)
        real, imag = product(matrix(0, rows), matrix(1, rows), vec_real, vec_imag)
        target[0] = real.astype(BF16)
        target[1] = imag.astype(BF16)


def join(level, half, keep, recv, joined):
    bit = bit_of(level)
    joined[:, pl.ds(pl.multiple_of(bit * half, half), half)] = keep[...]
    joined[:, pl.ds(pl.multiple_of((1 - bit) * half, half), half)] = recv[...]


def first_kernel(density, projection, transfers, low, keep, send, stage, dens_buf, proj_buf, sems):
    copies = [
        pltpu.make_async_copy(projection, proj_buf, sems.at[0]),
        pltpu.make_async_copy(density.at[0], dens_buf.at[0], sems.at[1]),
        pltpu.make_async_copy(density.at[1], dens_buf.at[1], sems.at[2]),
        pltpu.make_async_copy(transfers.at[0], stage, sems.at[3]),
    ]
    for copy in copies:
        copy.start()
    copies[1].wait()
    low[0] = dens_buf[0].astype(BF16)
    copies[2].wait()
    low[1] = dens_buf[1].astype(BF16)
    copies[0].wait()
    half = proj_buf.shape[1] // 2
    store_halves(0, half, lambda part, rows: proj_buf[part, rows], low[0], low[1], keep, send)
    copies[3].wait()


def level_kernel(level, keep, recv, transfers, keep_out, send_out, joined):
    half = keep.shape[1]
    join(level, half, keep, recv, joined)
    store_halves(
        level + 1,
        half,
        lambda part, rows: transfers[min(level, transfers.shape[0] - 1), part, rows],
        joined[0],
        joined[1],
        keep_out,
        send_out,
    )


def near_kernel(near_blocks, low, recv, interpolation, out, turned):
    for part in range(2):
        turned[part] = jnp.transpose(interpolation[part])
    odd = bit_of(0)
    beside = 2 - odd
    for vec, block, fresh in ((low, 0, True), (recv, beside, False)):
        real, imag = product(near_blocks[block, 0], near_blocks[block, 1], vec[0], vec[1])
        if fresh:
            out[0] = real
            out[1] = imag
        else:
            out[0] += real
            out[1] += imag


def far_near_kernel(near_blocks, recv, near, out):
    across = 1 + bit_of(0)
    real, imag = product(near_blocks[across, 0], near_blocks[across, 1], recv[0], recv[1])
    out[0] = near[0] + real
    out[1] = near[1] + imag


def last_kernel(level, keep, recv, transfers, interpolation, near, precondition, out, joined, result, sems):
    half = keep.shape[1]
    join(level, half, keep, recv, joined)
    real, imag = product(transfers[level, 0], transfers[level, 1], joined[0], joined[1])
    real, imag = real.astype(BF16), imag.astype(BF16)
    pre = jnp.transpose(precondition[...])
    rows = near.shape[1]
    parts = 3
    step = rows // parts
    copies = []
    for part in range(parts):
        span = pl.ds(part * step, step)
        far_real, far_imag = product(interpolation[0, span], interpolation[1, span], real, imag)
        total_real = near[0, span] + far_real
        total_imag = near[1, span] + far_imag
        pre_real = pre[part * step : (part + 1) * step, 0:1]
        pre_imag = pre[part * step : (part + 1) * step, 1:2]
        result[0, span] = pre_real * total_real - pre_imag * total_imag
        result[1, span] = pre_real * total_imag + pre_imag * total_real
        copy = pltpu.make_async_copy(result.at[:, span], out.at[:, span], sems.at[part])
        copy.start()
        copies.append(copy)
    for copy in copies:
        copy.wait()


def body(density, near_blocks, projection, transfers, interpolation, precondition):
    rows, angles = density.shape[1:]
    rank = projection.shape[1]
    half = rank // 2
    levels = transfers.shape[0]
    block = pltpu.VMEM((2, half, angles), BF16)
    whole = pltpu.VMEM((2, rows, angles), F32)
    low16 = pltpu.VMEM((2, rows, angles), BF16)
    low, keep, send, stage = call(
        first_kernel,
        "first",
        4,
        (low16, block, block, pltpu.VMEM((2, rank, rank), BF16)),
        (density, projection, transfers),
        in_specs=[HBM] * 3,
        scratch=[
            pltpu.VMEM(density.shape, F32),
            pltpu.VMEM(projection.shape, BF16),
            pltpu.SemaphoreType.DMA((4,)),
        ],
    )
    joined = pltpu.VMEM((2, rank, angles), BF16)
    transfers, near_blocks = held(transfers), held(near_blocks)
    for level in range(levels):
        recv = swapped(send, 1 << level)
        if level == 1:
            beside = swapped(low, 1)
        if level == 2:
            across = swapped_across(low)
            near, turned = call(
                near_kernel,
                "near",
                4,
                (whole, pltpu.VMEM((2, rows, rank), BF16)),
                (near_blocks, low, beside, jnp.swapaxes(interpolation, 1, 2)),
            )
        if level == 3:
            near = call(far_near_kernel, "near2", 4, whole, (near_blocks, across, near))
        if level == levels - 1:
            break
        keep, send = call(
            lambda *refs, level=level: level_kernel(level, *refs),
            f"level{level}",
            2,
            (block, block),
            (keep, recv, transfers if level else stage[None]),
            scratch=[joined],
        )
    return call(
        lambda *refs: last_kernel(levels - 1, *refs),
        "last",
        4,
        jax.ShapeDtypeStruct((2, rows, angles), F32),
        (keep, recv, transfers, turned, near, precondition),
        out_specs=HBM,
        scratch=[joined, pltpu.VMEM((2, rows, angles), F32), pltpu.SemaphoreType.DMA((3,))],
    )


def solution(mesh):
    placed = (
        P(None, "seg", None),
        P(None, None, "seg", None),
        P(None, "seg", None),
        P(None, None, "seg", None),
        P(None, "seg", None),
        P(None, "seg"),
    )
    return jax.shard_map(
        body, mesh=mesh, in_specs=placed, out_specs=P(None, "seg", None), check_vma=False
    )
```

time: 72 us -> 49.9 us (0.69)
  the two profiles are of different devices: /device:TPU:8 before, /device:TPU:2 now
where the time goes in v1:
time: 49.9 us; the launch traced here: 49.6 us
  starting transfers between devices  29.1 us (58%)
  waiting for transfers between devices  14.4 us (29%)
  Pallas kernels  5.89 us (12%)
    ppermute x6, starting transfers between devices, swapped(): lax.ppermute(array, 'seg', [(i, i ^ mask) for i in range(lax.axis_size('s...  24.9 us
    ppermute x6, waiting for transfers between devices, swapped(): lax.ppermute(array, 'seg', [(i, i ^ mask) for i in range(lax.axis_size('s...  14.4 us
    pallas_call x8, Pallas kernels, call(): pl.pallas_call(kernel, out_shape=out_shape, in_specs=in_specs or [VMEM] *...  5.89 us
    ppermute x1, starting transfers between devices, swapped_across(): lax.ppermute(array, 'seg', [(i, ((i + 1 ^ 1) - 1) % size) for i in range(...  4.16 us
  transfers between devices with their start and end apart: 7, of which 4 were waited for; matrix products, arithmetic and copies ran while one was open for 0% of the time, Pallas kernels for 5%

profile of v1, /device:TPU:2, one launch (start us, length us, event | category | flops | bytes accessed | tf_op | source)
XLA Modules:
  0.0 49.6 jit_solution(13698701013855461886)
XLA Ops:
  0.0 1.7 %first.1 = (bf16[2,384,256]{2,1,0:T(8,128)(2,1)S(1)}, bf16[2,96,256]{2,1,0:T(8,128)(2,1)S(1)}, bf16[2,96,256]{2,1,0:T(8,128)(2,1)S(1)}, bf16[2,192,192]{2,1,0:T(8,128)(2,1)S(1)}) custom-call(f32[2,384,256]{2,1,0:T(8,128)} %density.1, bf16[2,192,384]{2,1,0:T(8,128)(2,1)} %projection.1, bf16[5,2,192,192]{3,2,1,0:T(8,128)(2,1)} %refs_2_.7), custom_call_target="tpu_custom_call" | custom-call | tf_op jit(solution)/shard_map/first/pallas_call | solution.py:32
  1.7 1.9 %collective-permute-start = (bf16[2,96,256]{2,1,0:T(8,128)(2,1)S(1)}, bf16[2,96,256]{2,1,0:T(8,128)(2,1)S(1)}, u32[]{:S(2)}, u32[]{:S(2)}) collective-permute-start(bf16[2,96,256]{2,1,0:T(8,128)(2,1)S(1)} %get-tuple-element.20), channel_id=1, source_target_pairs={{0,1},{1,0},{2,3},{3,2},{4,5},{5,4},{6,7},{7,6},{8,9},{9,8},{10,11... | collective-permute-start | bytes 294920 | tf_op jit(solution)/shard_map/ppermute | solution.py:15
  3.7 1.3 %collective-permute-done.refs_1_ = bf16[2,96,256]{2,1,0:T(8,128)(2,1)S(1)} collective-permute-done((bf16[2,96,256]{2,1,0:T(8,128)(2,1)S(1)}, bf16[2,96,256]{2,1,0:T(8,128)(2,1)S(1)}, u32[]{:S(2)}, u32[]{:S(2)}) %collective-permute-start) | collective-permute-done | bytes 98336 | tf_op jit(solution)/shard_map/ppermute | solution.py:15
  4.9 0.3 level0.1
  5.2 3.5 %collective-permute-start.1 = (bf16[2,96,256]{2,1,0:T(8,128)(2,1)S(1)}, bf16[2,96,256]{2,1,0:T(8,128)(2,1)S(1)}, u32[]{:S(2)}, u32[]{:S(2)}) collective-permute-start(bf16[2,96,256]{2,1,0:T(8,128)(2,1)S(1)} %get-tuple-element.23), channel_id=1, source_target_pairs={{0,2},{1,3},{2,0},{3,1},{4,6},{5,7},{6,4},{7,5},{8,10},{9,11},{10,... | collective-permute-start | bytes 294920 | tf_op jit(solution)/shard_map/ppermute | solution.py:15
  8.7 1.9 %collective-permute-start.5 = (bf16[2,384,256]{2,1,0:T(8,128)(2,1)S(1)}, bf16[2,384,256]{2,1,0:T(8,128)(2,1)S(1)}, u32[]{:S(2)}, u32[]{:S(2)}) collective-permute-start(bf16[2,384,256]{2,1,0:T(8,128)(2,1)S(1)} %get-tuple-element.30.low), channel_id=1, source_target_pairs={{0,1},{1,0},{2,3},{3,2},{4,5},{5,4},{6,7},{7,6},{8,9},{9,8},{10,11... | collective-permute-start | bytes 1179656 | tf_op jit(solution)/shard_map/ppermute | solution.py:15
  10.6 4.2 %collective-permute-start.6 = (bf16[2,384,256]{2,1,0:T(8,128)(2,1)S(1)}, bf16[2,384,256]{2,1,0:T(8,128)(2,1)S(1)}, u32[]{:S(2)}, u32[]{:S(2)}) collective-permute-start(bf16[2,384,256]{2,1,0:T(8,128)(2,1)S(1)} %get-tuple-element.30.low), channel_id=1, source_target_pairs={{0,511},{1,2},{2,1},{3,4},{4,3},{5,6},{6,5},{7,8},{8,7},{9,10},{10... | collective-permute-start | bytes 1179656 | tf_op jit(solution)/shard_map/ppermute | solution.py:20
  14.8 0.0 collective-permute-done.1.refs_1_
  14.8 0.0 copy-start.1
  14.8 0.0 copy-start.2
  14.9 0.3 level1.1
  15.1 2.7 %collective-permute-start.2 = (bf16[2,96,256]{2,1,0:T(8,128)(2,1)S(1)}, bf16[2,96,256]{2,1,0:T(8,128)(2,1)S(1)}, u32[]{:S(2)}, u32[]{:S(2)}) collective-permute-start(bf16[2,96,256]{2,1,0:T(8,128)(2,1)S(1)} %get-tuple-element.25), channel_id=1, source_target_pairs={{0,4},{1,5},{2,6},{3,7},{4,0},{5,1},{6,2},{7,3},{8,12},{9,13},{10,... | collective-permute-start | bytes 294920 | tf_op jit(solution)/shard_map/ppermute | solution.py:15
  17.9 6.1 %collective-permute-done.2.refs_1_ = bf16[2,96,256]{2,1,0:T(8,128)(2,1)S(1)} collective-permute-done((bf16[2,96,256]{2,1,0:T(8,128)(2,1)S(1)}, bf16[2,96,256]{2,1,0:T(8,128)(2,1)S(1)}, u32[]{:S(2)}, u32[]{:S(2)}) %collective-permute-start.2) | collective-permute-done | bytes 98336 | tf_op jit(solution)/shard_map/ppermute | solution.py:15
  24.0 0.3 level2.1
  24.2 12.9 %collective-permute-start.3 = (bf16[2,96,256]{2,1,0:T(8,128)(2,1)S(1)}, bf16[2,96,256]{2,1,0:T(8,128)(2,1)S(1)}, u32[]{:S(2)}, u32[]{:S(2)}) collective-permute-start(bf16[2,96,256]{2,1,0:T(8,128)(2,1)S(1)} %get-tuple-element.27), channel_id=1, source_target_pairs={{0,8},{1,9},{2,10},{3,11},{4,12},{5,13},{6,14},{7,15},{8,0},{9,1},... | collective-permute-start | bytes 294920 | tf_op jit(solution)/shard_map/ppermute | solution.py:15
  37.2 2.6 %collective-permute-done.3.refs_1_ = bf16[2,96,256]{2,1,0:T(8,128)(2,1)S(1)} collective-permute-done((bf16[2,96,256]{2,1,0:T(8,128)(2,1)S(1)}, bf16[2,96,256]{2,1,0:T(8,128)(2,1)S(1)}, u32[]{:S(2)}, u32[]{:S(2)}) %collective-permute-start.3) | collective-permute-done | bytes 98336 | tf_op jit(solution)/shard_map/ppermute | solution.py:15
  39.8 0.3 level3.1
  40.1 1.9 %collective-permute-start.4 = (bf16[2,96,256]{2,1,0:T(8,128)(2,1)S(1)}, bf16[2,96,256]{2,1,0:T(8,128)(2,1)S(1)}, u32[]{:S(2)}, u32[]{:S(2)}) collective-permute-start(bf16[2,96,256]{2,1,0:T(8,128)(2,1)S(1)} %get-tuple-element.29), channel_id=1, source_target_pairs={{0,16},{1,17},{2,18},{3,19},{4,20},{5,21},{6,22},{7,23},{8,24},{9,... | collective-permute-start | bytes 294920 | tf_op jit(solution)/shard_map/ppermute | solution.py:15
  42.0 1.0 %near.1 = (f32[2,384,256]{2,1,0:T(8,128)S(1)}, bf16[2,384,192]{2,1,0:T(8,128)(2,1)S(1)}) custom-call(bf16[3,2,384,384]{3,2,1,0:T(8,128)(2,1)S(1)} %copy-done.1, bf16[2,384,256]{2,1,0:T(8,128)(2,1)S(1)} %get-tuple-element.30.low, bf16[2,384,256]{2,1,0:T(8,128)(2,1)S(1)} %collective-permute-done.5.recv, bf16[2,192,384]{2,1,0:T(8,128)(2,1)S(1)} %bitcast.2), custom_call_target="tpu_custom_call" | custom-call | tf_op jit(solution)/shard_map/near/pallas_call | solution.py:32
  43.0 0.0 collective-permute-done.6.recv
  43.0 0.0 copy-start.3
  43.0 0.6 %near2.1.refs_4_ = f32[2,384,256]{2,1,0:T(8,128)S(1)} custom-call(bf16[3,2,384,384]{3,2,1,0:T(8,128)(2,1)S(1)} %copy-done.1, bf16[2,384,256]{2,1,0:T(8,128)(2,1)S(1)} %collective-permute-done.6.recv, f32[2,384,256]{2,1,0:T(8,128)S(1)} %get-tuple-element.32.near), custom_call_target="tpu_custom_call" | custom-call | tf_op jit(solution)/shard_map/near2/pallas_call | solution.py:32
  43.6 4.5 %collective-permute-done.4.refs_1_ = bf16[2,96,256]{2,1,0:T(8,128)(2,1)S(1)} collective-permute-done((bf16[2,96,256]{2,1,0:T(8,128)(2,1)S(1)}, bf16[2,96,256]{2,1,0:T(8,128)(2,1)S(1)}, u32[]{:S(2)}, u32[]{:S(2)}) %collective-permute-start.4) | collective-permute-done | bytes 98336 | tf_op jit(solution)/shard_map/ppermute | solution.py:15
  48.1 1.5 %last.1 = f32[2,384,256]{2,1,0:T(8,128)} custom-call(bf16[2,96,256]{2,1,0:T(8,128)(2,1)S(1)} %get-tuple-element.28.refs_0_, bf16[2,96,256]{2,1,0:T(8,128)(2,1)S(1)} %collective-permute-done.4.refs_1_, bf16[5,2,192,192]{3,2,1,0:T(8,128)(2,1)S(1)} %copy-done, bf16[2,384,192]{2,1,0:T(8,128)(2,1)S(1)} %get-tuple-element.31.refs_3_, ...), custom_call_target="tpu_custom_call" | custom-call | tf_op jit(solution)/shard_map/last/pallas_call | solution.py:32
  (6 shorter events, 0.0 us)
Async XLA Ops:
  0.0 14.8 %copy-start = (bf16[5,2,192,192]{3,2,1,0:T(8,128)(2,1)S(1)}, bf16[5,2,192,192]{3,2,1,0:T(8,128)(2,1)}, u32[]{:S(2)}) copy-start(bf16[5,2,192,192]{3,2,1,0:T(8,128)(2,1)} %refs_2_.7) | copy-start | bytes 2211844
  1.7 3.2 %collective-permute-start = (bf16[2,96,256]{2,1,0:T(8,128)(2,1)S(1)}, bf16[2,96,256]{2,1,0:T(8,128)(2,1)S(1)}, u32[]{:S(2)}, u32[]{:S(2)}) collective-permute-start(bf16[2,96,256]{2,1,0:T(8,128)(2,1)S(1)} %get-tuple-element.20), channel_id=1, source_target_pairs={{0,1},{1,0},{2,3},{3,2},{4,5},{5,4},{6,7},{7,6},{8,9},{9,8},{10,11... | collective-permute-start | bytes 294920 | tf_op jit(solution)/shard_map/ppermute | solution.py:15
  5.2 9.6 %collective-permute-start.1 = (bf16[2,96,256]{2,1,0:T(8,128)(2,1)S(1)}, bf16[2,96,256]{2,1,0:T(8,128)(2,1)S(1)}, u32[]{:S(2)}, u32[]{:S(2)}) collective-permute-start(bf16[2,96,256]{2,1,0:T(8,128)(2,1)S(1)} %get-tuple-element.23), channel_id=1, source_target_pairs={{0,2},{1,3},{2,0},{3,1},{4,6},{5,7},{6,4},{7,5},{8,10},{9,11},{10,... | collective-permute-start | bytes 294920 | tf_op jit(solution)/shard_map/ppermute | solution.py:15
  8.7 33.3 %collective-permute-start.5 = (bf16[2,384,256]{2,1,0:T(8,128)(2,1)S(1)}, bf16[2,384,256]{2,1,0:T(8,128)(2,1)S(1)}, u32[]{:S(2)}, u32[]{:S(2)}) collective-permute-start(bf16[2,384,256]{2,1,0:T(8,128)(2,1)S(1)} %get-tuple-element.30.low), channel_id=1, source_target_pairs={{0,1},{1,0},{2,3},{3,2},{4,5},{5,4},{6,7},{7,6},{8,9},{9,8},{10,11... | collective-permute-start | bytes 1179656 | tf_op jit(solution)/shard_map/ppermute | solution.py:15
  10.6 32.4 %collective-permute-start.6 = (bf16[2,384,256]{2,1,0:T(8,128)(2,1)S(1)}, bf16[2,384,256]{2,1,0:T(8,128)(2,1)S(1)}, u32[]{:S(2)}, u32[]{:S(2)}) collective-permute-start(bf16[2,384,256]{2,1,0:T(8,128)(2,1)S(1)} %get-tuple-element.30.low), channel_id=1, source_target_pairs={{0,511},{1,2},{2,1},{3,4},{4,3},{5,6},{6,5},{7,8},{8,7},{9,10},{10... | collective-permute-start | bytes 1179656 | tf_op jit(solution)/shard_map/ppermute | solution.py:20
  14.8 27.2 %copy-start.1 = (bf16[3,2,384,384]{3,2,1,0:T(8,128)(2,1)S(1)}, bf16[3,2,384,384]{3,2,1,0:T(8,128)(2,1)}, u32[]{:S(2)}) copy-start(bf16[3,2,384,384]{3,2,1,0:T(8,128)(2,1)} %near_blocks.3) | copy-start | bytes 5308420
  14.8 27.2 %copy-start.2 = (bf16[2,384,192]{1,2,0:T(8,128)(2,1)S(1)}, bf16[2,384,192]{1,2,0:T(8,128)(2,1)}, u32[]{:S(2)}) copy-start(bf16[2,384,192]{1,2,0:T(8,128)(2,1)} %param.10) | copy-start | bytes 884740
  15.1 8.8 %collective-permute-start.2 = (bf16[2,96,256]{2,1,0:T(8,128)(2,1)S(1)}, bf16[2,96,256]{2,1,0:T(8,128)(2,1)S(1)}, u32[]{:S(2)}, u32[]{:S(2)}) collective-permute-start(bf16[2,96,256]{2,1,0:T(8,128)(2,1)S(1)} %get-tuple-element.25), channel_id=1, source_target_pairs={{0,4},{1,5},{2,6},{3,7},{4,0},{5,1},{6,2},{7,3},{8,12},{9,13},{10,... | collective-permute-start | bytes 294920 | tf_op jit(solution)/shard_map/ppermute | solution.py:15
  24.2 15.5 %collective-permute-start.3 = (bf16[2,96,256]{2,1,0:T(8,128)(2,1)S(1)}, bf16[2,96,256]{2,1,0:T(8,128)(2,1)S(1)}, u32[]{:S(2)}, u32[]{:S(2)}) collective-permute-start(bf16[2,96,256]{2,1,0:T(8,128)(2,1)S(1)} %get-tuple-element.27), channel_id=1, source_target_pairs={{0,8},{1,9},{2,10},{3,11},{4,12},{5,13},{6,14},{7,15},{8,0},{9,1},... | collective-permute-start | bytes 294920 | tf_op jit(solution)/shard_map/ppermute | solution.py:15
  40.1 8.0 %collective-permute-start.4 = (bf16[2,96,256]{2,1,0:T(8,128)(2,1)S(1)}, bf16[2,96,256]{2,1,0:T(8,128)(2,1)S(1)}, u32[]{:S(2)}, u32[]{:S(2)}) collective-permute-start(bf16[2,96,256]{2,1,0:T(8,128)(2,1)S(1)} %get-tuple-element.29), channel_id=1, source_target_pairs={{0,16},{1,17},{2,18},{3,19},{4,20},{5,21},{6,22},{7,23},{8,24},{9,... | collective-permute-start | bytes 294920 | tf_op jit(solution)/shard_map/ppermute | solution.py:15
  43.0 5.1 %copy-start.3 = (f32[2,384]{1,0:T(2,128)S(1)}, f32[2,384]{1,0:T(2,128)}, u32[]{:S(2)}) copy-start(f32[2,384]{1,0:T(2,128)} %refs_5_.1) | copy-start | bytes 9220

commit v2 on v1

v2 whole, which is shorter than its diff:
```python
import jax
import jax.numpy as jnp
from jax import lax
from jax.experimental import pallas as pl
from jax.experimental.pallas import tpu as pltpu
from jax.sharding import PartitionSpec as P


VMEM = pl.BlockSpec(memory_space=pltpu.VMEM)
HBM = pl.BlockSpec(memory_space=pltpu.HBM)
ANY = pl.BlockSpec(memory_space=pl.ANY)
F32 = jnp.float32
BF16 = jnp.bfloat16


def swapped(array, mask):
    return lax.ppermute(array, "seg", [(i, i ^ mask) for i in range(lax.axis_size("seg"))])


def swapped_across(array):
    size = lax.axis_size("seg")
    return lax.ppermute(array, "seg", [(i, ((i + 1) ^ 1) - 1) for i in range(1, size - 1)])


def moved(array, source, target):
    return lax.ppermute(array, "seg", [(source, target)])


def groups_of_four(level):
    low, high = 1 << level, 2 << level
    firsts = [i for i in range(lax.axis_size("seg")) if not i & (low | high)]
    return [[i, i | low, i | high, i | low | high] for i in firsts]


def held(array):
    return pltpu.with_memory_space_constraint(array, pltpu.VMEM)


def in_hbm(array):
    return pltpu.with_memory_space_constraint(array, pltpu.HBM)


PLACE = {pltpu.HBM: in_hbm, pltpu.VMEM: held, pl.ANY: lambda array: array}


def call(kernel, limit, out_shape, operands, in_specs=None, out_specs=None, scratch=(), aliases={}):
    in_specs = in_specs or [VMEM] * len(operands)
    return pl.pallas_call(
        kernel,
        out_shape=out_shape,
        in_specs=in_specs,
        out_specs=out_specs or jax.tree.map(lambda _: VMEM, out_shape),
        scratch_shapes=scratch,
        input_output_aliases=aliases,
        compiler_params=pltpu.CompilerParams(vmem_limit_bytes=limit << 20),
    )(*(PLACE[spec.memory_space](a) for a, spec in zip(operands, in_specs)))


def dot(left, right):
    return jnp.dot(left, right, preferred_element_type=F32)


def bit_of(level):
    return jnp.bitwise_and(jnp.right_shift(lax.axis_index("seg"), level), 1)


def product(real, imag, vec_real, vec_imag):
    return (
        dot(real, vec_real) - dot(imag, vec_imag),
        dot(real, vec_imag) + dot(imag, vec_real),
    )


def store_halves(level, half, matrix, vec_real, vec_imag, keep, send):
    bit = bit_of(level)
    for target, which in ((send, 1 - bit), (keep, bit)):
        rows = pl.ds(pl.multiple_of(which * half, half), half)
        real, imag = product(matrix(0, rows), matrix(1, rows), vec_real, vec_imag)
        target[0] = real.astype(BF16)
        target[1] = imag.astype(BF16)


def join(level, half, keep, recv, joined):
    bit = bit_of(level)
    joined[:, pl.ds(pl.multiple_of(bit * half, half), half)] = keep[...]
    joined[:, pl.ds(pl.multiple_of((1 - bit) * half, half), half)] = recv[...]


def half_rows(which, half):
    return pl.ds(pl.multiple_of(which * half, half), half)


def first_kernel(
    density,
    projection,
    transfers,
    low,
    keep,
    send,
    matrix0,
    matrix1,
    matrix2,
    dens_buf,
    proj_buf,
    sems,
):
    half = proj_buf.shape[1] // 2
    copies = [
        pltpu.make_async_copy(projection, proj_buf, sems.at[0]),
        pltpu.make_async_copy(density.at[0], dens_buf.at[0], sems.at[1]),
        pltpu.make_async_copy(density.at[1], dens_buf.at[1], sems.at[2]),
        pltpu.make_async_copy(transfers.at[0], matrix0.at[:, 0 : 2 * half], sems.at[3]),
        pltpu.make_async_copy(transfers.at[1], matrix1, sems.at[4]),
        pltpu.make_async_copy(transfers.at[2], matrix2, sems.at[5]),
        pltpu.make_async_copy(transfers.at[3, :, half_rows(1 - bit_of(4), half)], matrix0.at[:, 2 * half :], sems.at[6]),
    ]
    for copy in copies:
        copy.start()
    copies[1].wait()
    low[0] = dens_buf[0].astype(BF16)
    copies[2].wait()
    low[1] = dens_buf[1].astype(BF16)
    copies[0].wait()
    store_halves(0, half, lambda part, rows: proj_buf[part, rows], low[0], low[1], keep, send)
    for copy in copies[3:]:
        copy.wait()


def level_kernel(level, keep, recv, matrix, keep_out, send_out, joined):
    half = keep.shape[1]
    join(level, half, keep, recv, joined)
    store_halves(
        level + 1, half, lambda part, rows: matrix[part, rows], joined[0], joined[1], keep_out, send_out
    )


def level0_kernel(keep, recv, matrix, keep_out, send_out, rows3, joined):
    level_kernel(0, keep, recv, matrix, keep_out, send_out, joined)
    rows3[...] = matrix[:, matrix.shape[2] :]


def spread_kernel(level, keep, recv, matrix, out, joined, result, sems):
    half = keep.shape[1]
    join(level, half, keep, recv, joined)
    copies = []
    for which in range(2):
        rows = pl.ds(which * half, half)
        real, imag = product(matrix[0, rows], matrix[1, rows], joined[0], joined[1])
        result[which, 0] = real.astype(BF16)
        result[which, 1] = imag.astype(BF16)
        for member in (which, which + 2):
            copy = pltpu.make_async_copy(result.at[which], out.at[member], sems.at[member])
            copy.start()
            copies.append(copy)
    for copy in copies:
        copy.wait()


def join_four(level, recv, rows_own, rows_other, pair, joined):
    half = recv.shape[2]
    bit = bit_of(level + 1)
    pair[bit] = rows_own[...]
    pair[1 - bit] = rows_other[...]
    for side in range(2):
        vecs = [
            jnp.concatenate([recv[2 * side, part], recv[2 * side + 1, part]]) for part in range(2)
        ]
        real, imag = product(pair[side, 0], pair[side, 1], *vecs)
        joined[0, pl.ds(side * half, half)] = real.astype(BF16)
        joined[1, pl.ds(side * half, half)] = imag.astype(BF16)


def near_kernel(here, *refs):
    @pl.when((lax.axis_index("seg") == 0) == here)
    def _():
        near_work(here, *refs)


def near_work(
    here,
    near_blocks,
    interpolation,
    transfers,
    precondition,
    low,
    beside,
    across,
    *refs,
):
    out, turned, own3, matrix4, scales, buf, flat, vec_buf, sems = refs[-9:]
    half = own3.shape[1]
    odd = bit_of(0)
    order = ((0, low), (2 - odd, beside), (1 + odd, vec_buf if here else across))
    copies = [
        pltpu.make_async_copy(near_blocks.at[block], buf.at[i], sems.at[i])
        for i, (block, _) in enumerate(order)
    ]
    copies += [
        pltpu.make_async_copy(interpolation, flat, sems.at[3]),
        pltpu.make_async_copy(transfers.at[3, :, half_rows(bit_of(4), half)], own3, sems.at[4]),
        pltpu.make_async_copy(transfers.at[4], matrix4, sems.at[5]),
        pltpu.make_async_copy(precondition, scales, sems.at[6]),
    ]
    if here:
        copies.append(pltpu.make_async_copy(across, vec_buf, sems.at[7]))
    for copy in copies:
        copy.start()
    for i, (_, vec) in enumerate(order):
        copies[i].wait()
        if i == 2 and here:
            copies[7].wait()
        real, imag = product(buf[i, 0], buf[i, 1], vec[0], vec[1])
        if i:
            out[0] += real
            out[1] += imag
        else:
            out[0] = real
            out[1] = imag
    for copy in copies[3:7]:
        copy.wait()
    for part in range(2):
        turned[part] = jnp.transpose(flat[part])


def weighted(pre, real, imag):
    return pre[:, 0:1] * real - pre[:, 1:2] * imag, pre[:, 0:1] * imag + pre[:, 1:2] * real


def at_final():
    return lax.axis_index("seg") == lax.axis_size("seg") - 1


def finish_kernel(out_before, result, block, precondition, from_first, out, buf, sems):
    @pl.when(at_final())
    def _():
        pre = jnp.transpose(precondition[...])
        copies = []
        for part, span in enumerate(parts_of(result.shape[1])):
            real, imag = product(block[0, span], block[1, span], from_first[0], from_first[1])
            real, imag = weighted(pre[span], real, imag)
            buf[0, span] = result[0, span] + real
            buf[1, span] = result[1, span] + imag
            copy = pltpu.make_async_copy(buf.at[:, span], out.at[:, span], sems.at[part])
            copy.start()
            copies.append(copy)
        for copy in copies:
            copy.wait()


def parts_of(rows):
    step = rows // 3
    return [slice(part * step, (part + 1) * step) for part in range(3)]


def last_kernel(
    level,
    near_blocks,
    recv,
    rows_own,
    rows_other,
    matrix,
    interpolation,
    near,
    precondition,
    out,
    result,
    block,
    pair,
    joined,
    sems,
):
    fetch = pltpu.make_async_copy(near_blocks.at[2], block, sems.at[3])
    pl.when(at_final())(fetch.start)
    pre = jnp.transpose(precondition[...])
    join_four(level - 1, recv, rows_own, rows_other, pair, joined)
    real, imag = product(matrix[0], matrix[1], joined[0], joined[1])
    real, imag = real.astype(BF16), imag.astype(BF16)
    copies = []
    for part, span in enumerate(parts_of(near.shape[1])):
        far_real, far_imag = product(interpolation[0, span], interpolation[1, span], real, imag)
        result[0, span], result[1, span] = weighted(
            pre[span], near[0, span] + far_real, near[1, span] + far_imag
        )
        copy = pltpu.make_async_copy(result.at[:, span], out.at[:, span], sems.at[part])
        copy.start()
        copies.append(copy)
    for copy in copies:
        copy.wait()
    pl.when(at_final())(fetch.wait)


def body(density, near_blocks, projection, transfers, interpolation, precondition):
    rows, angles = density.shape[1:]
    rank = projection.shape[1]
    half = rank // 2
    levels = transfers.shape[0]
    block = pltpu.VMEM((2, half, angles), BF16)
    whole = pltpu.VMEM((2, rows, angles), F32)
    low16 = pltpu.VMEM((2, rows, angles), BF16)
    square = pltpu.VMEM((2, rank, rank), BF16)
    rows_half = pltpu.VMEM((2, half, rank), BF16)
    low, keep, send, matrix0, matrix1, matrix2 = call(
        first_kernel,
        4,
        (
            low16,
            block,
            block,
            pltpu.VMEM((2, rank + half, rank), BF16),
            square,
            square,
        ),
        (density, projection, transfers),
        in_specs=[HBM] * 3,
        scratch=[
            pltpu.VMEM(density.shape, F32),
            pltpu.VMEM(projection.shape, BF16),
            pltpu.SemaphoreType.DMA((7,)),
        ],
    )
    joined = pltpu.VMEM((2, rank, angles), BF16)
    pair = pltpu.VMEM((2, 2, half, rank), BF16)
    recv = swapped(send, 1)
    keep, send, rows3 = call(
        level0_kernel, 2, (block, block, rows_half), (keep, recv, matrix0), scratch=[joined]
    )
    recv = swapped(send, 2)
    keep, send = call(
        lambda *refs: level_kernel(1, *refs),
        2,
        (block, block),
        (keep, recv, matrix1),
        scratch=[joined],
    )
    recv = swapped(send, 4)
    rows3 = swapped(rows3, 16)
    beside = swapped(low, 1)
    across = swapped_across(low)
    final = lax.axis_size("seg") - 1
    from_final = moved(low, final, 0)
    from_first = moved(low, 0, final)
    send = call(
        lambda *refs: spread_kernel(2, *refs),
        2,
        jax.ShapeDtypeStruct((4, 2, half, angles), BF16),
        (keep, recv, matrix2),
        out_specs=HBM,
        scratch=[
            joined,
            pltpu.VMEM((2, 2, half, angles), BF16),
            pltpu.SemaphoreType.DMA((4,)),
        ],
    )
    recv = lax.all_to_all(send, "seg", 0, 0, axis_index_groups=groups_of_four(3))
    work = (whole, pltpu.VMEM((2, rows, rank), BF16), rows_half, square, pltpu.VMEM((2, rows), F32))
    done = ()
    for here in (True, False):
        done = call(
            lambda *refs, here=here: near_kernel(here, *refs),
            6,
            work,
            (
                near_blocks,
                jnp.swapaxes(interpolation, 1, 2),
                transfers,
                precondition,
                low,
                beside,
                from_final if here else across,
                *done,
            ),
            in_specs=[HBM] * 4 + [VMEM] * 2 + [ANY if here else VMEM] + [VMEM] * len(done),
            scratch=[
                pltpu.VMEM(near_blocks.shape, BF16),
                pltpu.VMEM((2, rank, rows), BF16),
                pltpu.VMEM(low.shape, BF16),
                pltpu.SemaphoreType.DMA((8,)),
            ],
            aliases={7 + k: k for k in range(len(done))},
        )
    near, turned, own3, matrix4, scales = done
    out = jax.ShapeDtypeStruct((2, rows, angles), F32)
    out, result, last_block = call(
        lambda *refs: last_kernel(levels - 1, *refs),
        6,
        (out, whole, pltpu.VMEM(near_blocks.shape[1:], BF16)),
        (near_blocks, recv, own3, rows3, matrix4, turned, near, scales),
        in_specs=[HBM] + [VMEM] * 7,
        out_specs=[HBM, VMEM, VMEM],
        scratch=[pair, joined, pltpu.SemaphoreType.DMA((4,))],
    )
    return call(
        finish_kernel,
        4,
        jax.ShapeDtypeStruct((2, rows, angles), F32),
        (out, result, last_block, scales, from_first),
        in_specs=[HBM] + [VMEM] * 4,
        out_specs=HBM,
        scratch=[pltpu.VMEM((2, rows, angles), F32), pltpu.SemaphoreType.DMA((3,))],
        aliases={0: 0},
    )


def solution(mesh):
    placed = (
        P(None, "seg", None),
        P(None, None, "seg", None),
        P(None, "seg", None),
        P(None, None, "seg", None),
        P(None, "seg", None),
        P(None, "seg"),
    )

    return jax.shard_map(
        body, mesh=mesh, in_specs=placed, out_specs=P(None, "seg", None), check_vma=False
    )
```

time: 49.9 us -> 51 us (1.022)
  waiting for transfers between devices: 14.4 us -> 7.13 us
  starting transfers between devices: 29.1 us -> 33.7 us
  Pallas kernels: 5.89 us -> 9.67 us
    all_to_all x0 -> x1, starting transfers between devices: none -> 13.6 us  [body(): lax.all_to_all(send, 'seg', 0, 0, axis_index_groups=groups_of_four(3))]
    ppermute x6 -> x5, starting transfers between devices: 24.9 us -> 13.8 us  [swapped(): lax.ppermute(array, 'seg', [(i, i ^ mask) for i in range(lax.axis_size('s...]
    ppermute x6 -> x5, waiting for transfers between devices: 14.4 us -> 7.12 us  [swapped(): lax.ppermute(array, 'seg', [(i, i ^ mask) for i in range(lax.axis_size('s...]
    pallas_call x8, Pallas kernels: 5.89 us -> 9.67 us  [call(): pl.pallas_call(kernel, out_shape=out_shape, in_specs=in_specs, out_specs=...]
    ppermute x1 -> x3, starting transfers between devices: 4.16 us -> 6.26 us  [the longest x1 4.16 us: swapped_across(): lax.ppermute(array, 'seg', [(i, (i + 1 ^ 1) - 1) for i in range(1, size -...]
  transfers between devices with their start and end apart: 7 -> 9, of which waited for: 4 -> 3; matrix products, arithmetic and copies ran while one was open for 0% -> 0% of each run, Pallas kernels for 5% -> 12%
where the time goes in v2:
time: 51 us; the launch traced here: 50.6 us
  starting transfers between devices  33.7 us (66%)
  Pallas kernels  9.67 us (19%)
  waiting for transfers between devices  7.13 us (14%)
    ppermute x5, starting transfers between devices, swapped(): lax.ppermute(array, 'seg', [(i, i ^ mask) for i in range(lax.axis_size('s...  13.8 us
    all_to_all x1, starting transfers between devices, body(): lax.all_to_all(send, 'seg', 0, 0, axis_index_groups=groups_of_four(3))  13.6 us
    pallas_call x8, Pallas kernels, call(): pl.pallas_call(kernel, out_shape=out_shape, in_specs=in_specs, out_specs=...  9.67 us
    ppermute x5, waiting for transfers between devices, swapped(): lax.ppermute(array, 'seg', [(i, i ^ mask) for i in range(lax.axis_size('s...  7.12 us
    ppermute x1, starting transfers between devices, swapped_across(): lax.ppermute(array, 'seg', [(i, (i + 1 ^ 1) - 1) for i in range(1, size -...  4.16 us
    ppermute x2, starting transfers between devices, moved(): return lax.ppermute(array, 'seg', [(source, target)])  2.1 us
  transfers between devices with their start and end apart: 9, of which 3 were waited for; matrix products, arithmetic and copies ran while one was open for 0% of the time, Pallas kernels for 12%

profile of v2, /device:TPU:2, one launch (start us, length us, event | category | flops | bytes accessed | tf_op | source)
XLA Modules:
  0.0 50.6 jit_solution(7025156424343143857)
XLA Ops:
  0.0 1.7 %shard_map.64 = (bf16[2,384,256]{2,1,0:T(8,128)(2,1)S(1)}, bf16[2,96,256]{2,1,0:T(8,128)(2,1)S(1)}, bf16[2,96,256]{2,1,0:T(8,128)(2,1)S(1)}, bf16[2,288,192]{2,1...) custom-call(f32[2,384,256]{2,1,0:T(8,128)} %density.1, ...), custom_call_target="tpu_custom_call" | custom-call | tf_op jit(solution)/shard_map/pallas_call | solution.py:48
  1.7 1.9 %collective-permute-start = (bf16[2,96,256]{2,1,0:T(8,128)(2,1)S(1)}, bf16[2,96,256]{2,1,0:T(8,128)(2,1)S(1)}, u32[]{:S(2)}, u32[]{:S(2)}) collective-permute-start(bf16[2,96,256]{2,1,0:T(8,128)(2,1)S(1)} %get-tuple-element.30), channel_id=1, source_target_pairs={{0,1},{1,0},{2,3},{3,2},{4,5},{5,4},{6,7},{7,6},{8,9},{9,8},{10,11... | collective-permute-start | bytes 294920 | tf_op jit(solution)/shard_map/ppermute | solution.py:17
  3.6 1.3 %collective-permute-done.recv = bf16[2,96,256]{2,1,0:T(8,128)(2,1)S(1)} collective-permute-done((bf16[2,96,256]{2,1,0:T(8,128)(2,1)S(1)}, bf16[2,96,256]{2,1,0:T(8,128)(2,1)S(1)}, u32[]{:S(2)}, u32[]{:S(2)}) %collective-permute-start) | collective-permute-done | bytes 98336 | tf_op jit(solution)/shard_map/ppermute | solution.py:17
  4.9 0.9 %shard_map.65 = (bf16[2,96,256]{2,1,0:T(8,128)(2,1)S(1)}, bf16[2,96,256]{2,1,0:T(8,128)(2,1)S(1)}, bf16[2,96,192]{2,1,0:T(8,128)(2,1)}) custom-call(bf16[2,96,256]{2,1,0:T(8,128)(2,1)S(1)} %get-tuple-element.29.keep, bf16[2,96,256]{2,1,0:T(8,128)(2,1)S(1)} %collective-permute-done.recv, bf16[2,288,192]{2,1,0:T(8,128)(2,1)S(1)} %get-tuple-element.31.matrix), custom_call_target="tpu_custom_call" | custom-call | tf_op jit(solution)/shard_map/pallas_call | solution.py:48
  5.7 3.5 %collective-permute-start.1 = (bf16[2,96,256]{2,1,0:T(8,128)(2,1)S(1)}, bf16[2,96,256]{2,1,0:T(8,128)(2,1)S(1)}, u32[]{:S(2)}, u32[]{:S(2)}) collective-permute-start(bf16[2,96,256]{2,1,0:T(8,128)(2,1)S(1)} %get-tuple-element.33), channel_id=1, source_target_pairs={{0,2},{1,3},{2,0},{3,1},{4,6},{5,7},{6,4},{7,5},{8,10},{9,11},{10,... | collective-permute-start | bytes 294920 | tf_op jit(solution)/shard_map/ppermute | solution.py:17
  9.2 1.9 %collective-permute-start.3 = (bf16[2,384,256]{2,1,0:T(8,128)(2,1)S(1)}, bf16[2,384,256]{2,1,0:T(8,128)(2,1)S(1)}, u32[]{:S(2)}, u32[]{:S(2)}) collective-permute-start(bf16[2,384,256]{2,1,0:T(8,128)(2,1)S(1)} %get-tuple-element.38.refs_4_), channel_id=1, source_target_pairs={{0,1},{1,0},{2,3},{3,2},{4,5},{5,4},{6,7},{7,6},{8,9},{9,8},{10,11... | collective-permute-start | bytes 1179656 | tf_op jit(solution)/shard_map/ppermute | solution.py:17
  11.1 0.7 %collective-permute-start.5 = (bf16[2,384,256]{2,1,0:T(8,128)(2,1)S(1)}, bf16[2,384,256]{2,1,0:T(8,128)(2,1)S(1)}, u32[]{:S(2)}, u32[]{:S(2)}) collective-permute-start(bf16[2,384,256]{2,1,0:T(8,128)(2,1)S(1)} %get-tuple-element.38.refs_4_), channel_id=1, source_target_pairs={{511,0}} | collective-permute-start | bytes 1179656 | tf_op jit(solution)/shard_map/ppermute | solution.py:26
  11.8 4.2 %collective-permute-start.4 = (bf16[2,384,256]{2,1,0:T(8,128)(2,1)S(1)}, bf16[2,384,256]{2,1,0:T(8,128)(2,1)S(1)}, u32[]{:S(2)}, u32[]{:S(2)}) collective-permute-start(bf16[2,384,256]{2,1,0:T(8,128)(2,1)S(1)} %get-tuple-element.38.refs_4_), channel_id=1, source_target_pairs={{1,2},{2,1},{3,4},{4,3},{5,6},{6,5},{7,8},{8,7},{9,10},{10,9},{11,... | collective-permute-start | bytes 1179656 | tf_op jit(solution)/shard_map/ppermute | solution.py:22
  16.0 0.0 collective-permute-done.1.refs_1_
  16.0 0.3 shard_map.66
  16.3 2.6 %collective-permute-start.2 = (bf16[2,96,256]{2,1,0:T(8,128)(2,1)S(1)}, bf16[2,96,256]{2,1,0:T(8,128)(2,1)S(1)}, u32[]{:S(2)}, u32[]{:S(2)}) collective-permute-start(bf16[2,96,256]{2,1,0:T(8,128)(2,1)S(1)} %get-tuple-element.36), channel_id=1, source_target_pairs={{0,4},{1,5},{2,6},{3,7},{4,0},{5,1},{6,2},{7,3},{8,12},{9,13},{10,... | collective-permute-start | bytes 294920 | tf_op jit(solution)/shard_map/ppermute | solution.py:17
  18.9 1.4 %collective-permute-start.7 = (bf16[2,384,256]{2,1,0:T(8,128)(2,1)S(1)}, bf16[2,384,256]{2,1,0:T(8,128)(2,1)}, u32[]{:S(2)}, u32[]{:S(2)}) collective-permute-start(bf16[2,384,256]{2,1,0:T(8,128)(2,1)S(1)} %get-tuple-element.38.refs_4_), channel_id=1, source_target_pairs={{0,511}} | collective-permute-start | bytes 1179656 | tf_op jit(solution)/shard_map/ppermute | solution.py:26
  20.3 4.8 %collective-permute-done.2.refs_1_ = bf16[2,96,256]{2,1,0:T(8,128)(2,1)S(1)} collective-permute-done((bf16[2,96,256]{2,1,0:T(8,128)(2,1)S(1)}, bf16[2,96,256]{2,1,0:T(8,128)(2,1)S(1)}, u32[]{:S(2)}, u32[]{:S(2)}) %collective-permute-start.2) | collective-permute-done | bytes 98336 | tf_op jit(solution)/shard_map/ppermute | solution.py:17
  25.1 1.0 %shard_map.67 = bf16[4,2,96,256]{3,2,1,0:T(8,128)(2,1)} custom-call(bf16[2,96,256]{2,1,0:T(8,128)(2,1)S(1)} %get-tuple-element.35.refs_0_, bf16[2,96,256]{2,1,0:T(8,128)(2,1)S(1)} %collective-permute-done.2.refs_1_, bf16[2,192,192]{2,1,0:T(8,128)(2,1)S(1)} %get-tuple-element.37.refs_2_), custom_call_target="tpu_custom_call" | custom-call | tf_op jit(solution)/shard_map/pallas_call | solution.py:48
  26.2 13.6 %all-to-all-start = ((bf16[4,2,96,256]{3,2,1,0:T(8,128)(2,1)}), bf16[4,2,96,256]{3,2,1,0:T(8,128)(2,1)S(1)}, u32[]{:S(2)}, u32[]{:S(2)}) async-start(bf16[4,2,96,256]{3,2,1,0:T(8,128)(2,1)} %shard_map.67), calls=%async_computation | async-start | bytes 786432 | tf_op jit(solution)/shard_map/all_to_all | solution.py:354
  39.7 4.0 %collective-permute-start.6 = (bf16[2,96,192]{2,1,0:T(8,128)(2,1)}, bf16[2,96,192]{2,1,0:T(8,128)(2,1)S(1)}, u32[]{:S(2)}, u32[]{:S(2)}) collective-permute-start(bf16[2,96,192]{2,1,0:T(8,128)(2,1)} %get-tuple-element.45), channel_id=1, source_target_pairs={{0,16},{1,17},{2,18},{3,19},{4,20},{5,21},{6,22},{7,23},{8,24},{9,... | collective-permute-start | bytes 221192 | tf_op jit(solution)/shard_map/ppermute | solution.py:17
  43.7 0.0 collective-permute-done.3.refs_5_
  43.7 0.1 shard_map.68
  43.8 0.0 collective-permute-done.4.refs_6_
  43.8 3.1 %shard_map.69 = (f32[2,384,256]{2,1,0:T(8,128)S(1)}, bf16[2,384,192]{2,1,0:T(8,128)(2,1)S(1)}, bf16[2,96,192]{2,1,0:T(8,128)(2,1)S(1)}, bf16[2,192,192]{2,1,0:T(8,128)(2,1)S(1)}, f32[2,384]{1,0:T(2,128)S(1)}) custom-call(bf16[3,2,384,384]{3,2,1,0:T(8,128)(2,1)} %refs_0_.5, ...), custom_call_target="tpu_custom_call", output_to_operand_aliasing={{0}: (7, {}), {1}: (8, {}), {2}: (9, {}), {3}: (10, {}), {4... | custom-call | tf_op jit(solution)/shard_map/pallas_call | solution.py:48
  46.9 1.0 %collective-permute-done.6.refs_3_ = bf16[2,96,192]{2,1,0:T(8,128)(2,1)S(1)} collective-permute-done((bf16[2,96,192]{2,1,0:T(8,128)(2,1)}, bf16[2,96,192]{2,1,0:T(8,128)(2,1)S(1)}, u32[]{:S(2)}, u32[]{:S(2)}) %collective-permute-start.6) | collective-permute-done | bytes 73760 | tf_op jit(solution)/shard_map/ppermute | solution.py:17
  47.9 0.0 all-to-all-done.refs_1_
  47.9 1.6 %shard_map.70 = (f32[2,384,256]{2,1,0:T(8,128)}, f32[2,384,256]{2,1,0:T(8,128)S(1)}, bf16[2,384,384]{2,1,0:T(8,128)(2,1)S(1)}) custom-call(bf16[3,2,384,384]{3,2,1,0:T(8,128)(2,1)} %refs_0_.5, bf16[4,2,96,256]{3,2,1,0:T(8,128)(2,1)S(1)} %all-to-all-done.refs_1_, bf16[2,96,192]{2,1,0:T(8,128)(2,1)S(1)} %get-tuple-element.44.refs_2_, ...), custom_call_target="tpu_custom_call" | custom-call | tf_op jit(solution)/shard_map/pallas_call | solution.py:48
  49.6 1.0 %shard_map.71 = f32[2,384,256]{2,1,0:T(8,128)} custom-call(f32[2,384,256]{2,1,0:T(8,128)} %get-tuple-element.50.out_before, f32[2,384,256]{2,1,0:T(8,128)S(1)} %get-tuple-element.51.result, bf16[2,384,384]{2,1,0:T(8,128)(2,1)S(1)} %get-tuple-element.52.block, f32[2,384]{1,0:T(2,128)S(1)} %get-tuple-element.49.refs_7_.precondition, ...), custom_call_target="tpu_custom_call", output_to_operand_aliasing={{}: (0, {})} | custom-call | tf_op jit(solution)/shard_map/pallas_call | solution.py:48
  (2 shorter events, 0.0 us)
Async XLA Ops:
  1.7 3.2 %collective-permute-start = (bf16[2,96,256]{2,1,0:T(8,128)(2,1)S(1)}, bf16[2,96,256]{2,1,0:T(8,128)(2,1)S(1)}, u32[]{:S(2)}, u32[]{:S(2)}) collective-permute-start(bf16[2,96,256]{2,1,0:T(8,128)(2,1)S(1)} %get-tuple-element.30), channel_id=1, source_target_pairs={{0,1},{1,0},{2,3},{3,2},{4,5},{5,4},{6,7},{7,6},{8,9},{9,8},{10,11... | collective-permute-start | bytes 294920 | tf_op jit(solution)/shard_map/ppermute | solution.py:17
  5.7 10.3 %collective-permute-start.1 = (bf16[2,96,256]{2,1,0:T(8,128)(2,1)S(1)}, bf16[2,96,256]{2,1,0:T(8,128)(2,1)S(1)}, u32[]{:S(2)}, u32[]{:S(2)}) collective-permute-start(bf16[2,96,256]{2,1,0:T(8,128)(2,1)S(1)} %get-tuple-element.33), channel_id=1, source_target_pairs={{0,2},{1,3},{2,0},{3,1},{4,6},{5,7},{6,4},{7,5},{8,10},{9,11},{10,... | collective-permute-start | bytes 294920 | tf_op jit(solution)/shard_map/ppermute | solution.py:17
  9.2 34.5 %collective-permute-start.3 = (bf16[2,384,256]{2,1,0:T(8,128)(2,1)S(1)}, bf16[2,384,256]{2,1,0:T(8,128)(2,1)S(1)}, u32[]{:S(2)}, u32[]{:S(2)}) collective-permute-start(bf16[2,384,256]{2,1,0:T(8,128)(2,1)S(1)} %get-tuple-element.38.refs_4_), channel_id=1, source_target_pairs={{0,1},{1,0},{2,3},{3,2},{4,5},{5,4},{6,7},{7,6},{8,9},{9,8},{10,11... | collective-permute-start | bytes 1179656 | tf_op jit(solution)/shard_map/ppermute | solution.py:17
  11.1 32.6 %collective-permute-start.5 = (bf16[2,384,256]{2,1,0:T(8,128)(2,1)S(1)}, bf16[2,384,256]{2,1,0:T(8,128)(2,1)S(1)}, u32[]{:S(2)}, u32[]{:S(2)}) collective-permute-start(bf16[2,384,256]{2,1,0:T(8,128)(2,1)S(1)} %get-tuple-element.38.refs_4_), channel_id=1, source_target_pairs={{511,0}} | collective-permute-start | bytes 1179656 | tf_op jit(solution)/shard_map/ppermute | solution.py:26
  11.8 32.0 %collective-permute-start.4 = (bf16[2,384,256]{2,1,0:T(8,128)(2,1)S(1)}, bf16[2,384,256]{2,1,0:T(8,128)(2,1)S(1)}, u32[]{:S(2)}, u32[]{:S(2)}) collective-permute-start(bf16[2,384,256]{2,1,0:T(8,128)(2,1)S(1)} %get-tuple-element.38.refs_4_), channel_id=1, source_target_pairs={{1,2},{2,1},{3,4},{4,3},{5,6},{6,5},{7,8},{8,7},{9,10},{10,9},{11,... | collective-permute-start | bytes 1179656 | tf_op jit(solution)/shard_map/ppermute | solution.py:22
  16.3 8.8 %collective-permute-start.2 = (bf16[2,96,256]{2,1,0:T(8,128)(2,1)S(1)}, bf16[2,96,256]{2,1,0:T(8,128)(2,1)S(1)}, u32[]{:S(2)}, u32[]{:S(2)}) collective-permute-start(bf16[2,96,256]{2,1,0:T(8,128)(2,1)S(1)} %get-tuple-element.36), channel_id=1, source_target_pairs={{0,4},{1,5},{2,6},{3,7},{4,0},{5,1},{6,2},{7,3},{8,12},{9,13},{10,... | collective-permute-start | bytes 294920 | tf_op jit(solution)/shard_map/ppermute | solution.py:17
  18.9 30.7 %collective-permute-start.7 = (bf16[2,384,256]{2,1,0:T(8,128)(2,1)S(1)}, bf16[2,384,256]{2,1,0:T(8,128)(2,1)}, u32[]{:S(2)}, u32[]{:S(2)}) collective-permute-start(bf16[2,384,256]{2,1,0:T(8,128)(2,1)S(1)} %get-tuple-element.38.refs_4_), channel_id=1, source_target_pairs={{0,511}} | collective-permute-start | bytes 1179656 | tf_op jit(solution)/shard_map/ppermute | solution.py:26
  26.2 21.8 %all-to-all-start = ((bf16[4,2,96,256]{3,2,1,0:T(8,128)(2,1)}), bf16[4,2,96,256]{3,2,1,0:T(8,128)(2,1)S(1)}, u32[]{:S(2)}, u32[]{:S(2)}) async-start(bf16[4,2,96,256]{3,2,1,0:T(8,128)(2,1)} %shard_map.67), calls=%async_computation | async-start | bytes 786432 | tf_op jit(solution)/shard_map/all_to_all | solution.py:354
  39.7 8.2 %collective-permute-start.6 = (bf16[2,96,192]{2,1,0:T(8,128)(2,1)}, bf16[2,96,192]{2,1,0:T(8,128)(2,1)S(1)}, u32[]{:S(2)}, u32[]{:S(2)}) collective-permute-start(bf16[2,96,192]{2,1,0:T(8,128)(2,1)} %get-tuple-element.45), channel_id=1, source_target_pairs={{0,16},{1,17},{2,18},{3,19},{4,20},{5,21},{6,22},{7,23},{8,24},{9,... | collective-permute-start | bytes 221192 | tf_op jit(solution)/shard_map/ppermute | solution.py:17

commit v3 on v2

--- a/solution.py
+++ b/solution.py
@@ -96,7 +96,7 @@
     transfers,
     low,
     keep,
-    send,
+    packed,
     matrix0,
     matrix1,
     matrix2,
@@ -114,14 +114,22 @@
         pltpu.make_async_copy(transfers.at[2], matrix2, sems.at[5]),
         pltpu.make_async_copy(transfers.at[3, :, half_rows(1 - bit_of(4), half)], matrix0.at[:, 2 * half :], sems.at[6]),
     ]
-    for copy in copies:
-        copy.start()
-    copies[1].wait()
-    low[0] = dens_buf[0].astype(BF16)
-    copies[2].wait()
-    low[1] = dens_buf[1].astype(BF16)
+    for k in (1, 2, 0, 3, 4, 5, 6):
+        copies[k].start()
+    for part in range(2):
+        copies[part + 1].wait()
+        low[part] = dens_buf[part].astype(BF16)
+        packed[part, half:] = low[part]
     copies[0].wait()
-    store_halves(0, half, lambda part, rows: proj_buf[part, rows], low[0], low[1], keep, send)
+    store_halves(
+        0,
+        half,
+        lambda part, rows: proj_buf[part, rows],
+        low[0],
+        low[1],
+        keep,
+        packed.at[:, 0:half],
+    )
     for copy in copies[3:]:
         copy.wait()
 
@@ -135,7 +143,8 @@
 
 
 def level0_kernel(keep, recv, matrix, keep_out, send_out, rows3, joined):
-    level_kernel(0, keep, recv, matrix, keep_out, send_out, joined)
+    half = keep.shape[1]
+    level_kernel(0, keep, recv.at[:, 0:half], matrix, keep_out, send_out, joined)
     rows3[...] = matrix[:, matrix.shape[2] :]
 
 
@@ -156,11 +165,8 @@
         copy.wait()
 
 
-def join_four(level, recv, rows_own, rows_other, pair, joined):
+def join_four(recv, pair, joined):
     half = recv.shape[2]
-    bit = bit_of(level + 1)
-    pair[bit] = rows_own[...]
-    pair[1 - bit] = rows_other[...]
     for side in range(2):
         vecs = [
             jnp.concatenate([recv[2 * side, part], recv[2 * side + 1, part]]) for part in range(2)
@@ -173,42 +179,44 @@
 def near_kernel(here, *refs):
     @pl.when((lax.axis_index("seg") == 0) == here)
     def _():
-        near_work(here, *refs)
+        near_work(*refs)
 
 
 def near_work(
-    here,
     near_blocks,
     interpolation,
     transfers,
     precondition,
     low,
     beside,
+    rows3,
     across,
     *refs,
 ):
-    out, turned, own3, matrix4, scales, buf, flat, vec_buf, sems = refs[-9:]
-    half = own3.shape[1]
+    out, turned, pair, matrix4, scales, buf, flat, vec_buf, sems = refs[-9:]
+    half = pair.shape[2]
+    side = bit_of(4)
+    beside = beside.at[:, half:]
     odd = bit_of(0)
-    order = ((0, low), (2 - odd, beside), (1 + odd, vec_buf if here else across))
+    order = ((0, low), (2 - odd, beside), (1 + odd, vec_buf))
     copies = [
         pltpu.make_async_copy(near_blocks.at[block], buf.at[i], sems.at[i])
         for i, (block, _) in enumerate(order)
     ]
     copies += [
         pltpu.make_async_copy(interpolation, flat, sems.at[3]),
-        pltpu.make_async_copy(transfers.at[3, :, half_rows(bit_of(4), half)], own3, sems.at[4]),
+        pltpu.make_async_copy(transfers.at[3, :, half_rows(side, half)], pair.at[side], sems.at[4]),
+        pltpu.make_async_copy(rows3, pair.at[1 - side], sems.at[7]),
         pltpu.make_async_copy(transfers.at[4], matrix4, sems.at[5]),
         pltpu.make_async_copy(precondition, scales, sems.at[6]),
     ]
-    if here:
-        copies.append(pltpu.make_async_copy(across, vec_buf, sems.at[7]))
+    copies.append(pltpu.make_async_copy(across, vec_buf, sems.at[8]))
     for copy in copies:
         copy.start()
     for i, (_, vec) in enumerate(order):
         copies[i].wait()
-        if i == 2 and here:
-            copies[7].wait()
+        if i == 2:
+            copies[8].wait()
         real, imag = product(buf[i, 0], buf[i, 1], vec[0], vec[1])
         if i:
             out[0] += real
@@ -216,7 +224,7 @@
         else:
             out[0] = real
             out[1] = imag
-    for copy in copies[3:7]:
+    for copy in copies[3:8]:
         copy.wait()
     for part in range(2):
         turned[part] = jnp.transpose(flat[part])
@@ -253,11 +261,9 @@
 
 
 def last_kernel(
-    level,
     near_blocks,
     recv,
-    rows_own,
-    rows_other,
+    pair,
     matrix,
     interpolation,
     near,
@@ -265,14 +271,13 @@
     out,
     result,
     block,
-    pair,
     joined,
     sems,
 ):
     fetch = pltpu.make_async_copy(near_blocks.at[2], block, sems.at[3])
     pl.when(at_final())(fetch.start)
     pre = jnp.transpose(precondition[...])
-    join_four(level - 1, recv, rows_own, rows_other, pair, joined)
+    join_four(recv, pair, joined)
     real, imag = product(matrix[0], matrix[1], joined[0], joined[1])
     real, imag = real.astype(BF16), imag.astype(BF16)
     copies = []
@@ -293,19 +298,18 @@
     rows, angles = density.shape[1:]
     rank = projection.shape[1]
     half = rank // 2
-    levels = transfers.shape[0]
     block = pltpu.VMEM((2, half, angles), BF16)
     whole = pltpu.VMEM((2, rows, angles), F32)
     low16 = pltpu.VMEM((2, rows, angles), BF16)
     square = pltpu.VMEM((2, rank, rank), BF16)
     rows_half = pltpu.VMEM((2, half, rank), BF16)
-    low, keep, send, matrix0, matrix1, matrix2 = call(
+    low, keep, packed, matrix0, matrix1, matrix2 = call(
         first_kernel,
         4,
         (
             low16,
             block,
-            block,
+            pltpu.VMEM((2, half + rows, angles), BF16),
             pltpu.VMEM((2, rank + half, rank), BF16),
             square,
             square,
@@ -320,9 +324,9 @@
     )
     joined = pltpu.VMEM((2, rank, angles), BF16)
     pair = pltpu.VMEM((2, 2, half, rank), BF16)
-    recv = swapped(send, 1)
+    packed = swapped(packed, 1)
     keep, send, rows3 = call(
-        level0_kernel, 2, (block, block, rows_half), (keep, recv, matrix0), scratch=[joined]
+        level0_kernel, 2, (block, block, rows_half), (keep, packed, matrix0), scratch=[joined]
     )
     recv = swapped(send, 2)
     keep, send = call(
@@ -334,7 +338,6 @@
     )
     recv = swapped(send, 4)
     rows3 = swapped(rows3, 16)
-    beside = swapped(low, 1)
     across = swapped_across(low)
     final = lax.axis_size("seg") - 1
     from_final = moved(low, final, 0)
@@ -352,7 +355,7 @@
         ],
     )
     recv = lax.all_to_all(send, "seg", 0, 0, axis_index_groups=groups_of_four(3))
-    work = (whole, pltpu.VMEM((2, rows, rank), BF16), rows_half, square, pltpu.VMEM((2, rows), F32))
+    work = (whole, pltpu.VMEM((2, rows, rank), BF16), pair, square, pltpu.VMEM((2, rows), F32))
     done = ()
     for here in (True, False):
         done = call(
@@ -365,29 +368,30 @@
                 transfers,
                 precondition,
                 low,
-                beside,
+                packed,
+                rows3,
                 from_final if here else across,
                 *done,
             ),
-            in_specs=[HBM] * 4 + [VMEM] * 2 + [ANY if here else VMEM] + [VMEM] * len(done),
+            in_specs=[HBM] * 4 + [VMEM] * 2 + [ANY] * 2 + [VMEM] * len(done),
             scratch=[
                 pltpu.VMEM(near_blocks.shape, BF16),
                 pltpu.VMEM((2, rank, rows), BF16),
                 pltpu.VMEM(low.shape, BF16),
-                pltpu.SemaphoreType.DMA((8,)),
+                pltpu.SemaphoreType.DMA((9,)),
             ],
-            aliases={7 + k: k for k in range(len(done))},
+            aliases={8 + k: k for k in range(len(done))},
         )
-    near, turned, own3, matrix4, scales = done
+    near, turned, pair, matrix4, scales = done
     out = jax.ShapeDtypeStruct((2, rows, angles), F32)
     out, result, last_block = call(
-        lambda *refs: last_kernel(levels - 1, *refs),
+        last_kernel,
         6,
         (out, whole, pltpu.VMEM(near_blocks.shape[1:], BF16)),
-        (near_blocks, recv, own3, rows3, matrix4, turned, near, scales),
-        in_specs=[HBM] + [VMEM] * 7,
+        (near_blocks, recv, pair, matrix4, turned, near, scales),
+        in_specs=[HBM] + [VMEM] * 6,
         out_specs=[HBM, VMEM, VMEM],
-        scratch=[pair, joined, pltpu.SemaphoreType.DMA((4,))],
+        scratch=[joined, pltpu.SemaphoreType.DMA((4,))],
     )
     return call(
         finish_kernel,

time: 51 us -> 53.1 us (1.041)
  waiting for transfers between devices: 7.13 us -> 9.05 us
  local copies, waits for them, and re-layouts: 0 us -> 1.74 us
  starting transfers between devices: 33.7 us -> 32.7 us
  Pallas kernels: 9.67 us -> 9.07 us
    ppermute x5 -> x4, waiting for transfers between devices: 7.12 us -> 9.04 us  [swapped(): lax.ppermute(array, 'seg', [(i, i ^ mask) for i in range(lax.axis_size('s...]
    unnamed x0 -> x4, local copies, waits for them, and re-layouts: none -> 1.74 us
    ppermute x1, starting transfers between devices: 4.16 us -> 3.52 us  [swapped_across(): lax.ppermute(array, 'seg', [(i, (i + 1 ^ 1) - 1) for i in range(1, size -...]
    pallas_call x8, Pallas kernels: 9.67 us -> 9.07 us  [call(): pl.pallas_call(kernel, out_shape=out_shape, in_specs=in_specs, out_specs=...]
    ppermute x5 -> x4, starting transfers between devices: 13.8 us -> 13.5 us  [swapped(): lax.ppermute(array, 'seg', [(i, i ^ mask) for i in range(lax.axis_size('s...]
  transfers between devices with their start and end apart: 9 -> 8, of which waited for: 3 -> 3; matrix products, arithmetic and copies ran while one was open for 0% -> 0% of each run, Pallas kernels for 12% -> 12%
where the time goes in v3:
time: 53.1 us; the launch traced here: 52.7 us
  starting transfers between devices  32.7 us (62%)
  Pallas kernels  9.07 us (17%)
  waiting for transfers between devices  9.05 us (17%)
  local copies, waits for them, and re-layouts  1.74 us (3%)
    all_to_all x1, starting transfers between devices, body(): lax.all_to_all(send, 'seg', 0, 0, axis_index_groups=groups_of_four(3))  13.6 us
    ppermute x4, starting transfers between devices, swapped(): lax.ppermute(array, 'seg', [(i, i ^ mask) for i in range(lax.axis_size('s...  13.5 us
    pallas_call x8, Pallas kernels, call(): pl.pallas_call(kernel, out_shape=out_shape, in_specs=in_specs, out_specs=...  9.07 us
    ppermute x4, waiting for transfers between devices, swapped(): lax.ppermute(array, 'seg', [(i, i ^ mask) for i in range(lax.axis_size('s...  9.04 us
    ppermute x1, starting transfers between devices, swapped_across(): lax.ppermute(array, 'seg', [(i, (i + 1 ^ 1) - 1) for i in range(1, size -...  3.52 us
    ppermute x2, starting transfers between devices, moved(): return lax.ppermute(array, 'seg', [(source, target)])  2.11 us
    unnamed x4, local copies, waits for them, and re-layouts  1.74 us
  transfers between devices with their start and end apart: 8, of which 3 were waited for; matrix products, arithmetic and copies ran while one was open for 0% of the time, Pallas kernels for 12%

profile of v3, /device:TPU:2, one launch (start us, length us, event | category | flops | bytes accessed | tf_op | source)
XLA Modules:
  0.0 52.7 jit_solution(12314573965167466193)
XLA Ops:
  0.0 1.6 %shard_map.64 = (bf16[2,384,256]{2,1,0:T(8,128)(2,1)S(1)}, bf16[2,96,256]{2,1,0:T(8,128)(2,1)S(1)}, bf16[2,480,256]{2,1,0:T(8,128)(2,1)S(1)}, bf16[2,288,192]{2,...) custom-call(f32[2,384,256]{2,1,0:T(8,128)} %density.1, ...), custom_call_target="tpu_custom_call" | custom-call | tf_op jit(solution)/shard_map/pallas_call | solution.py:48
  1.7 1.9 %collective-permute-start = (bf16[2,480,256]{2,1,0:T(8,128)(2,1)S(1)}, bf16[2,480,256]{2,1,0:T(8,128)(2,1)S(1)}, u32[]{:S(2)}, u32[]{:S(2)}) collective-permute-start(bf16[2,480,256]{2,1,0:T(8,128)(2,1)S(1)} %get-tuple-element.30), channel_id=1, source_target_pairs={{0,1},{1,0},{2,3},{3,2},{4,5},{5,4},{6,7},{7,6},{8,9},{9,8},{10,11... | collective-permute-start | bytes 1474568 | tf_op jit(solution)/shard_map/ppermute | solution.py:17
  3.6 1.8 %collective-permute-done.recv.refs_5_ = bf16[2,480,256]{2,1,0:T(8,128)(2,1)S(1)} collective-permute-done((bf16[2,480,256]{2,1,0:T(8,128)(2,1)S(1)}, bf16[2,480,256]{2,1,0:T(8,128)(2,1)S(1)}, u32[]{:S(2)}, u32[]{:S(2)}) %collective-permute-start) | collective-permute-done | bytes 491552 | tf_op jit(solution)/shard_map/ppermute | solution.py:17
  5.4 0.3 shard_map.65
  5.7 3.5 %collective-permute-start.1 = (bf16[2,96,256]{2,1,0:T(8,128)(2,1)S(1)}, bf16[2,96,256]{2,1,0:T(8,128)(2,1)S(1)}, u32[]{:S(2)}, u32[]{:S(2)}) collective-permute-start(bf16[2,96,256]{2,1,0:T(8,128)(2,1)S(1)} %get-tuple-element.33), channel_id=1, source_target_pairs={{0,2},{1,3},{2,0},{3,1},{4,6},{5,7},{6,4},{7,5},{8,10},{9,11},{10,... | collective-permute-start | bytes 294920 | tf_op jit(solution)/shard_map/ppermute | solution.py:17
  9.2 0.7 %collective-permute-start.5 = (bf16[2,384,256]{2,1,0:T(8,128)(2,1)S(1)}, bf16[2,384,256]{2,1,0:T(8,128)(2,1)S(1)}, u32[]{:S(2)}, u32[]{:S(2)}) collective-permute-start(bf16[2,384,256]{2,1,0:T(8,128)(2,1)S(1)} %get-tuple-element.38.refs_4_), channel_id=1, source_target_pairs={{511,0}} | collective-permute-start | bytes 1179656 | tf_op jit(solution)/shard_map/ppermute | solution.py:26
  9.9 3.5 %collective-permute-start.4 = (bf16[2,384,256]{2,1,0:T(8,128)(2,1)S(1)}, bf16[2,384,256]{2,1,0:T(8,128)(2,1)S(1)}, u32[]{:S(2)}, u32[]{:S(2)}) collective-permute-start(bf16[2,384,256]{2,1,0:T(8,128)(2,1)S(1)} %get-tuple-element.38.refs_4_), channel_id=1, source_target_pairs={{1,2},{2,1},{3,4},{4,3},{5,6},{6,5},{7,8},{8,7},{9,10},{10,9},{11,... | collective-permute-start | bytes 1179656 | tf_op jit(solution)/shard_map/ppermute | solution.py:22
  13.4 0.0 collective-permute-done.1.refs_1_
  13.4 0.3 shard_map.66
  13.7 4.1 %collective-permute-start.2 = (bf16[2,96,256]{2,1,0:T(8,128)(2,1)S(1)}, bf16[2,96,256]{2,1,0:T(8,128)(2,1)S(1)}, u32[]{:S(2)}, u32[]{:S(2)}) collective-permute-start(bf16[2,96,256]{2,1,0:T(8,128)(2,1)S(1)} %get-tuple-element.36), channel_id=1, source_target_pairs={{0,4},{1,5},{2,6},{3,7},{4,0},{5,1},{6,2},{7,3},{8,12},{9,13},{10,... | collective-permute-start | bytes 294920 | tf_op jit(solution)/shard_map/ppermute | solution.py:17
  17.8 1.4 %collective-permute-start.6 = (bf16[2,384,256]{2,1,0:T(8,128)(2,1)S(1)}, bf16[2,384,256]{2,1,0:T(8,128)(2,1)}, u32[]{:S(2)}, u32[]{:S(2)}) collective-permute-start(bf16[2,384,256]{2,1,0:T(8,128)(2,1)S(1)} %get-tuple-element.38.refs_4_), channel_id=1, source_target_pairs={{0,511}} | collective-permute-start | bytes 1179656 | tf_op jit(solution)/shard_map/ppermute | solution.py:26
  19.3 3.9 %collective-permute-done.2.refs_1_ = bf16[2,96,256]{2,1,0:T(8,128)(2,1)S(1)} collective-permute-done((bf16[2,96,256]{2,1,0:T(8,128)(2,1)S(1)}, bf16[2,96,256]{2,1,0:T(8,128)(2,1)S(1)}, u32[]{:S(2)}, u32[]{:S(2)}) %collective-permute-start.2) | collective-permute-done | bytes 98336 | tf_op jit(solution)/shard_map/ppermute | solution.py:17
  23.2 1.0 %shard_map.67 = bf16[4,2,96,256]{3,2,1,0:T(8,128)(2,1)} custom-call(bf16[2,96,256]{2,1,0:T(8,128)(2,1)S(1)} %get-tuple-element.35.refs_0_, bf16[2,96,256]{2,1,0:T(8,128)(2,1)S(1)} %collective-permute-done.2.refs_1_, bf16[2,192,192]{2,1,0:T(8,128)(2,1)S(1)} %get-tuple-element.37.refs_2_), custom_call_target="tpu_custom_call" | custom-call | tf_op jit(solution)/shard_map/pallas_call | solution.py:48
  24.2 13.6 %all-to-all-start = ((bf16[4,2,96,256]{3,2,1,0:T(8,128)(2,1)}), bf16[4,2,96,256]{3,2,1,0:T(8,128)(2,1)S(1)}, u32[]{:S(2)}, u32[]{:S(2)}) async-start(bf16[4,2,96,256]{3,2,1,0:T(8,128)(2,1)} %shard_map.67), calls=%async_computation | async-start | bytes 786432 | tf_op jit(solution)/shard_map/all_to_all | solution.py:357
  37.8 4.0 %collective-permute-start.3 = (bf16[2,96,192]{2,1,0:T(8,128)(2,1)S(1)}, bf16[2,96,192]{2,1,0:T(8,128)(2,1)S(1)}, u32[]{:S(2)}, u32[]{:S(2)}) collective-permute-start(bf16[2,96,192]{2,1,0:T(8,128)(2,1)S(1)} %get-tuple-element.39), channel_id=1, source_target_pairs={{0,16},{1,17},{2,18},{3,19},{4,20},{5,21},{6,22},{7,23},{8,24},{9,... | collective-permute-start | bytes 221192 | tf_op jit(solution)/shard_map/ppermute | solution.py:17
  41.8 0.0 collective-permute-done.5.refs_7_
  41.8 0.7 %copy-done = bf16[2,384,256]{2,1,0:T(8,128)(2,1)} copy-done((bf16[2,384,256]{2,1,0:T(8,128)(2,1)}, bf16[2,384,256]{2,1,0:T(8,128)(2,1)S(1)}, u32[]{:S(2)}) %copy-start) | copy-done | bytes 393240
  42.5 3.3 %collective-permute-done.3.refs_6_ = bf16[2,96,192]{2,1,0:T(8,128)(2,1)S(1)} collective-permute-done((bf16[2,96,192]{2,1,0:T(8,128)(2,1)S(1)}, bf16[2,96,192]{2,1,0:T(8,128)(2,1)S(1)}, u32[]{:S(2)}, u32[]{:S(2)}) %collective-permute-start.3) | collective-permute-done | bytes 73760 | tf_op jit(solution)/shard_map/ppermute | solution.py:17
  45.8 1.0 %copy-done.1 = bf16[2,384,256]{2,1,0:T(8,128)(2,1)S(1)} copy-done((bf16[2,384,256]{2,1,0:T(8,128)(2,1)S(1)}, bf16[2,384,256]{2,1,0:T(8,128)(2,1)}, u32[]{:S(2)}) %copy-start.1) | copy-done | bytes 393240
  46.8 0.1 shard_map.68
  46.9 0.0 collective-permute-done.4.refs_7_
  46.9 3.1 %shard_map.69 = (f32[2,384,256]{2,1,0:T(8,128)S(1)}, bf16[2,384,192]{2,1,0:T(8,128)(2,1)S(1)}, bf16[2,2,96,192]{3,2,1,0:T(8,128)(2,1)S(1)}, bf16[2,192,192]{2,1,0:T(8,128)(2,1)S(1)}, f32[2,384]{1,0:T(2,128)S(1)}) custom-call(bf16[3,2,384,384]{3,2,1,0:T(8,128)(2,1)} %near_blocks.1, ...), custom_call_target="tpu_custom_call", output_to_operand_aliasing={{0}: (8, {}), {1}: (9, {}), {2}: (10, {}), {3}: (11, {}), {... | custom-call | tf_op jit(solution)/shard_map/pallas_call | solution.py:48
  50.0 1.6 %shard_map.70 = (f32[2,384,256]{2,1,0:T(8,128)}, f32[2,384,256]{2,1,0:T(8,128)S(1)}, bf16[2,384,384]{2,1,0:T(8,128)(2,1)S(1)}) custom-call(bf16[3,2,384,384]{3,2,1,0:T(8,128)(2,1)} %near_blocks.1, bf16[4,2,96,256]{3,2,1,0:T(8,128)(2,1)S(1)} %all-to-all-done.recv, bf16[2,2,96,192]{3,2,1,0:T(8,128)(2,1)S(1)} %get-tuple-element.45.pair, ...), custom_call_target="tpu_custom_call" | custom-call | tf_op jit(solution)/shard_map/pallas_call | solution.py:48
  51.7 1.0 %shard_map.71 = f32[2,384,256]{2,1,0:T(8,128)} custom-call(f32[2,384,256]{2,1,0:T(8,128)} %get-tuple-element.50.out_before, f32[2,384,256]{2,1,0:T(8,128)S(1)} %get-tuple-element.51.result, bf16[2,384,384]{2,1,0:T(8,128)(2,1)S(1)} %get-tuple-element.52.block, f32[2,384]{1,0:T(2,128)S(1)} %get-tuple-element.49.precondition, ...), custom_call_target="tpu_custom_call", output_to_operand_aliasing={{}: (0, {})} | custom-call | tf_op jit(solution)/shard_map/pallas_call | solution.py:48
  (4 shorter events, 0.0 us)
Async XLA Ops:
  1.7 3.8 %collective-permute-start = (bf16[2,480,256]{2,1,0:T(8,128)(2,1)S(1)}, bf16[2,480,256]{2,1,0:T(8,128)(2,1)S(1)}, u32[]{:S(2)}, u32[]{:S(2)}) collective-permute-start(bf16[2,480,256]{2,1,0:T(8,128)(2,1)S(1)} %get-tuple-element.30), channel_id=1, source_target_pairs={{0,1},{1,0},{2,3},{3,2},{4,5},{5,4},{6,7},{7,6},{8,9},{9,8},{10,11... | collective-permute-start | bytes 1474568 | tf_op jit(solution)/shard_map/ppermute | solution.py:17
  5.7 7.7 %collective-permute-start.1 = (bf16[2,96,256]{2,1,0:T(8,128)(2,1)S(1)}, bf16[2,96,256]{2,1,0:T(8,128)(2,1)S(1)}, u32[]{:S(2)}, u32[]{:S(2)}) collective-permute-start(bf16[2,96,256]{2,1,0:T(8,128)(2,1)S(1)} %get-tuple-element.33), channel_id=1, source_target_pairs={{0,2},{1,3},{2,0},{3,1},{4,6},{5,7},{6,4},{7,5},{8,10},{9,11},{10,... | collective-permute-start | bytes 294920 | tf_op jit(solution)/shard_map/ppermute | solution.py:17
  9.2 32.6 %collective-permute-start.5 = (bf16[2,384,256]{2,1,0:T(8,128)(2,1)S(1)}, bf16[2,384,256]{2,1,0:T(8,128)(2,1)S(1)}, u32[]{:S(2)}, u32[]{:S(2)}) collective-permute-start(bf16[2,384,256]{2,1,0:T(8,128)(2,1)S(1)} %get-tuple-element.38.refs_4_), channel_id=1, source_target_pairs={{511,0}} | collective-permute-start | bytes 1179656 | tf_op jit(solution)/shard_map/ppermute | solution.py:26
  9.9 37.0 %collective-permute-start.4 = (bf16[2,384,256]{2,1,0:T(8,128)(2,1)S(1)}, bf16[2,384,256]{2,1,0:T(8,128)(2,1)S(1)}, u32[]{:S(2)}, u32[]{:S(2)}) collective-permute-start(bf16[2,384,256]{2,1,0:T(8,128)(2,1)S(1)} %get-tuple-element.38.refs_4_), channel_id=1, source_target_pairs={{1,2},{2,1},{3,4},{4,3},{5,6},{6,5},{7,8},{8,7},{9,10},{10,9},{11,... | collective-permute-start | bytes 1179656 | tf_op jit(solution)/shard_map/ppermute | solution.py:22
  13.7 9.5 %collective-permute-start.2 = (bf16[2,96,256]{2,1,0:T(8,128)(2,1)S(1)}, bf16[2,96,256]{2,1,0:T(8,128)(2,1)S(1)}, u32[]{:S(2)}, u32[]{:S(2)}) collective-permute-start(bf16[2,96,256]{2,1,0:T(8,128)(2,1)S(1)} %get-tuple-element.36), channel_id=1, source_target_pairs={{0,4},{1,5},{2,6},{3,7},{4,0},{5,1},{6,2},{7,3},{8,12},{9,13},{10,... | collective-permute-start | bytes 294920 | tf_op jit(solution)/shard_map/ppermute | solution.py:17
  17.8 33.8 %collective-permute-start.6 = (bf16[2,384,256]{2,1,0:T(8,128)(2,1)S(1)}, bf16[2,384,256]{2,1,0:T(8,128)(2,1)}, u32[]{:S(2)}, u32[]{:S(2)}) collective-permute-start(bf16[2,384,256]{2,1,0:T(8,128)(2,1)S(1)} %get-tuple-element.38.refs_4_), channel_id=1, source_target_pairs={{0,511}} | collective-permute-start | bytes 1179656 | tf_op jit(solution)/shard_map/ppermute | solution.py:26
  24.2 25.8 %all-to-all-start = ((bf16[4,2,96,256]{3,2,1,0:T(8,128)(2,1)}), bf16[4,2,96,256]{3,2,1,0:T(8,128)(2,1)S(1)}, u32[]{:S(2)}, u32[]{:S(2)}) async-start(bf16[4,2,96,256]{3,2,1,0:T(8,128)(2,1)} %shard_map.67), calls=%async_computation | async-start | bytes 786432 | tf_op jit(solution)/shard_map/all_to_all | solution.py:357
  37.8 8.0 %collective-permute-start.3 = (bf16[2,96,192]{2,1,0:T(8,128)(2,1)S(1)}, bf16[2,96,192]{2,1,0:T(8,128)(2,1)S(1)}, u32[]{:S(2)}, u32[]{:S(2)}) collective-permute-start(bf16[2,96,192]{2,1,0:T(8,128)(2,1)S(1)} %get-tuple-element.39), channel_id=1, source_target_pairs={{0,16},{1,17},{2,18},{3,19},{4,20},{5,21},{6,22},{7,23},{8,24},{9,... | collective-permute-start | bytes 221192 | tf_op jit(solution)/shard_map/ppermute | solution.py:17
  41.8 0.8 %copy-start = (bf16[2,384,256]{2,1,0:T(8,128)(2,1)}, bf16[2,384,256]{2,1,0:T(8,128)(2,1)S(1)}, u32[]{:S(2)}) copy-start(bf16[2,384,256]{2,1,0:T(8,128)(2,1)S(1)} %collective-permute-done.5.refs_7_) | copy-start | bytes 1179652
  45.8 1.0 %copy-start.1 = (bf16[2,384,256]{2,1,0:T(8,128)(2,1)S(1)}, bf16[2,384,256]{2,1,0:T(8,128)(2,1)}, u32[]{:S(2)}) copy-start(bf16[2,384,256]{2,1,0:T(8,128)(2,1)} %copy-done) | copy-start | bytes 1179652

commit v4 on v3

--- a/solution.py
+++ b/solution.py
@@ -29,7 +29,7 @@
 def groups_of_four(level):
     low, high = 1 << level, 2 << level
     firsts = [i for i in range(lax.axis_size("seg")) if not i & (low | high)]
-    return [[i, i | low, i | high, i | low | high] for i in firsts]
+    return [[i | low | high, i | high, i | low, i] for i in firsts]
 
 
 def held(array):
@@ -157,7 +157,7 @@
         real, imag = product(matrix[0, rows], matrix[1, rows], joined[0], joined[1])
         result[which, 0] = real.astype(BF16)
         result[which, 1] = imag.astype(BF16)
-        for member in (which, which + 2):
+        for member in (1 - which, 3 - which):
             copy = pltpu.make_async_copy(result.at[which], out.at[member], sems.at[member])
             copy.start()
             copies.append(copy)
@@ -169,7 +169,8 @@
     half = recv.shape[2]
     for side in range(2):
         vecs = [
-            jnp.concatenate([recv[2 * side, part], recv[2 * side + 1, part]]) for part in range(2)
+            jnp.concatenate([recv[3 - 2 * side, part], recv[2 - 2 * side, part]])
+            for part in range(2)
         ]
         real, imag = product(pair[side, 0], pair[side, 1], *vecs)
         joined[0, pl.ds(side * half, half)] = real.astype(BF16)

time: 53.1 us -> 53 us (level)
  starting transfers between devices: 32.7 us -> 30.5 us
  waiting for transfers between devices: 9.05 us -> 11.1 us
    ppermute x4, starting transfers between devices: 13.5 us -> 11.4 us  [swapped(): lax.ppermute(array, 'seg', [(i, i ^ mask) for i in range(lax.axis_size('s...]
    ppermute x4, waiting for transfers between devices: 9.04 us -> 11.1 us  [swapped(): lax.ppermute(array, 'seg', [(i, i ^ mask) for i in range(lax.axis_size('s...]
where the time goes in v4:
time: 53 us; the launch traced here: 52.6 us
  starting transfers between devices  30.5 us (58%)
  waiting for transfers between devices  11.1 us (21%)
  Pallas kernels  9.07 us (17%)
  local copies, waits for them, and re-layouts  1.74 us (3%)
    all_to_all x1, starting transfers between devices, body(): lax.all_to_all(send, 'seg', 0, 0, axis_index_groups=groups_of_four(3))  13.5 us
    ppermute x4, starting transfers between devices, swapped(): lax.ppermute(array, 'seg', [(i, i ^ mask) for i in range(lax.axis_size('s...  11.4 us
    ppermute x4, waiting for transfers between devices, swapped(): lax.ppermute(array, 'seg', [(i, i ^ mask) for i in range(lax.axis_size('s...  11.1 us
    pallas_call x8, Pallas kernels, call(): pl.pallas_call(kernel, out_shape=out_shape, in_specs=in_specs, out_specs=...  9.07 us
    ppermute x1, starting transfers between devices, swapped_across(): lax.ppermute(array, 'seg', [(i, (i + 1 ^ 1) - 1) for i in range(1, size -...  3.52 us
    ppermute x2, starting transfers between devices, moved(): return lax.ppermute(array, 'seg', [(source, target)])  2.11 us
    unnamed x4, local copies, waits for them, and re-layouts  1.74 us
  transfers between devices with their start and end apart: 8, of which 3 were waited for; matrix products, arithmetic and copies ran while one was open for 0% of the time, Pallas kernels for 12%

profile of v4, /device:TPU:2, one launch (start us, length us, event | category | flops | bytes accessed | tf_op | source)
XLA Modules:
  0.0 52.6 jit_solution(14605685636603686677)
XLA Ops:
  0.0 1.6 %shard_map.64 = (bf16[2,384,256]{2,1,0:T(8,128)(2,1)S(1)}, bf16[2,96,256]{2,1,0:T(8,128)(2,1)S(1)}, bf16[2,480,256]{2,1,0:T(8,128)(2,1)S(1)}, bf16[2,288,192]{2,...) custom-call(f32[2,384,256]{2,1,0:T(8,128)} %density.1, ...), custom_call_target="tpu_custom_call" | custom-call | tf_op jit(solution)/shard_map/pallas_call | solution.py:48
  1.7 1.9 %collective-permute-start = (bf16[2,480,256]{2,1,0:T(8,128)(2,1)S(1)}, bf16[2,480,256]{2,1,0:T(8,128)(2,1)S(1)}, u32[]{:S(2)}, u32[]{:S(2)}) collective-permute-start(bf16[2,480,256]{2,1,0:T(8,128)(2,1)S(1)} %get-tuple-element.30), channel_id=1, source_target_pairs={{0,1},{1,0},{2,3},{3,2},{4,5},{5,4},{6,7},{7,6},{8,9},{9,8},{10,11... | collective-permute-start | bytes 1474568 | tf_op jit(solution)/shard_map/ppermute | solution.py:17
  3.6 1.8 %collective-permute-done.recv.refs_5_ = bf16[2,480,256]{2,1,0:T(8,128)(2,1)S(1)} collective-permute-done((bf16[2,480,256]{2,1,0:T(8,128)(2,1)S(1)}, bf16[2,480,256]{2,1,0:T(8,128)(2,1)S(1)}, u32[]{:S(2)}, u32[]{:S(2)}) %collective-permute-start) | collective-permute-done | bytes 491552 | tf_op jit(solution)/shard_map/ppermute | solution.py:17
  5.4 0.3 shard_map.65
  5.7 3.5 %collective-permute-start.1 = (bf16[2,96,256]{2,1,0:T(8,128)(2,1)S(1)}, bf16[2,96,256]{2,1,0:T(8,128)(2,1)S(1)}, u32[]{:S(2)}, u32[]{:S(2)}) collective-permute-start(bf16[2,96,256]{2,1,0:T(8,128)(2,1)S(1)} %get-tuple-element.33), channel_id=1, source_target_pairs={{0,2},{1,3},{2,0},{3,1},{4,6},{5,7},{6,4},{7,5},{8,10},{9,11},{10,... | collective-permute-start | bytes 294920 | tf_op jit(solution)/shard_map/ppermute | solution.py:17
  9.2 0.7 %collective-permute-start.5 = (bf16[2,384,256]{2,1,0:T(8,128)(2,1)S(1)}, bf16[2,384,256]{2,1,0:T(8,128)(2,1)S(1)}, u32[]{:S(2)}, u32[]{:S(2)}) collective-permute-start(bf16[2,384,256]{2,1,0:T(8,128)(2,1)S(1)} %get-tuple-element.38.refs_4_), channel_id=1, source_target_pairs={{511,0}} | collective-permute-start | bytes 1179656 | tf_op jit(solution)/shard_map/ppermute | solution.py:26
  9.9 3.5 %collective-permute-start.4 = (bf16[2,384,256]{2,1,0:T(8,128)(2,1)S(1)}, bf16[2,384,256]{2,1,0:T(8,128)(2,1)S(1)}, u32[]{:S(2)}, u32[]{:S(2)}) collective-permute-start(bf16[2,384,256]{2,1,0:T(8,128)(2,1)S(1)} %get-tuple-element.38.refs_4_), channel_id=1, source_target_pairs={{1,2},{2,1},{3,4},{4,3},{5,6},{6,5},{7,8},{8,7},{9,10},{10,9},{11,... | collective-permute-start | bytes 1179656 | tf_op jit(solution)/shard_map/ppermute | solution.py:22
  13.4 0.0 collective-permute-done.1.refs_1_
  13.4 0.3 shard_map.66
  13.7 4.1 %collective-permute-start.2 = (bf16[2,96,256]{2,1,0:T(8,128)(2,1)S(1)}, bf16[2,96,256]{2,1,0:T(8,128)(2,1)S(1)}, u32[]{:S(2)}, u32[]{:S(2)}) collective-permute-start(bf16[2,96,256]{2,1,0:T(8,128)(2,1)S(1)} %get-tuple-element.36), channel_id=1, source_target_pairs={{0,4},{1,5},{2,6},{3,7},{4,0},{5,1},{6,2},{7,3},{8,12},{9,13},{10,... | collective-permute-start | bytes 294920 | tf_op jit(solution)/shard_map/ppermute | solution.py:17
  17.8 1.4 %collective-permute-start.6 = (bf16[2,384,256]{2,1,0:T(8,128)(2,1)S(1)}, bf16[2,384,256]{2,1,0:T(8,128)(2,1)}, u32[]{:S(2)}, u32[]{:S(2)}) collective-permute-start(bf16[2,384,256]{2,1,0:T(8,128)(2,1)S(1)} %get-tuple-element.38.refs_4_), channel_id=1, source_target_pairs={{0,511}} | collective-permute-start | bytes 1179656 | tf_op jit(solution)/shard_map/ppermute | solution.py:26
  19.3 3.9 %collective-permute-done.2.refs_1_ = bf16[2,96,256]{2,1,0:T(8,128)(2,1)S(1)} collective-permute-done((bf16[2,96,256]{2,1,0:T(8,128)(2,1)S(1)}, bf16[2,96,256]{2,1,0:T(8,128)(2,1)S(1)}, u32[]{:S(2)}, u32[]{:S(2)}) %collective-permute-start.2) | collective-permute-done | bytes 98336 | tf_op jit(solution)/shard_map/ppermute | solution.py:17
  23.2 1.0 %shard_map.67 = bf16[4,2,96,256]{3,2,1,0:T(8,128)(2,1)} custom-call(bf16[2,96,256]{2,1,0:T(8,128)(2,1)S(1)} %get-tuple-element.35.refs_0_, bf16[2,96,256]{2,1,0:T(8,128)(2,1)S(1)} %collective-permute-done.2.refs_1_, bf16[2,192,192]{2,1,0:T(8,128)(2,1)S(1)} %get-tuple-element.37.refs_2_), custom_call_target="tpu_custom_call" | custom-call | tf_op jit(solution)/shard_map/pallas_call | solution.py:48
  24.2 13.5 %all-to-all-start = ((bf16[4,2,96,256]{3,2,1,0:T(8,128)(2,1)}), bf16[4,2,96,256]{3,2,1,0:T(8,128)(2,1)S(1)}, u32[]{:S(2)}, u32[]{:S(2)}) async-start(bf16[4,2,96,256]{3,2,1,0:T(8,128)(2,1)} %shard_map.67), calls=%async_computation | async-start | bytes 786432 | tf_op jit(solution)/shard_map/all_to_all | solution.py:358
  37.7 1.9 %collective-permute-start.3 = (bf16[2,96,192]{2,1,0:T(8,128)(2,1)S(1)}, bf16[2,96,192]{2,1,0:T(8,128)(2,1)S(1)}, u32[]{:S(2)}, u32[]{:S(2)}) collective-permute-start(bf16[2,96,192]{2,1,0:T(8,128)(2,1)S(1)} %get-tuple-element.39), channel_id=1, source_target_pairs={{0,16},{1,17},{2,18},{3,19},{4,20},{5,21},{6,22},{7,23},{8,24},{9,... | collective-permute-start | bytes 221192 | tf_op jit(solution)/shard_map/ppermute | solution.py:17
  39.6 0.0 collective-permute-done.5.refs_7_
  39.6 0.7 %copy-done = bf16[2,384,256]{2,1,0:T(8,128)(2,1)} copy-done((bf16[2,384,256]{2,1,0:T(8,128)(2,1)}, bf16[2,384,256]{2,1,0:T(8,128)(2,1)S(1)}, u32[]{:S(2)}) %copy-start) | copy-done | bytes 393240
  40.4 5.3 %collective-permute-done.3.refs_6_ = bf16[2,96,192]{2,1,0:T(8,128)(2,1)S(1)} collective-permute-done((bf16[2,96,192]{2,1,0:T(8,128)(2,1)S(1)}, bf16[2,96,192]{2,1,0:T(8,128)(2,1)S(1)}, u32[]{:S(2)}, u32[]{:S(2)}) %collective-permute-start.3) | collective-permute-done | bytes 73760 | tf_op jit(solution)/shard_map/ppermute | solution.py:17
  45.7 1.0 %copy-done.1 = bf16[2,384,256]{2,1,0:T(8,128)(2,1)S(1)} copy-done((bf16[2,384,256]{2,1,0:T(8,128)(2,1)S(1)}, bf16[2,384,256]{2,1,0:T(8,128)(2,1)}, u32[]{:S(2)}) %copy-start.1) | copy-done | bytes 393240
  46.7 0.1 shard_map.68
  46.8 3.1 %shard_map.69 = (f32[2,384,256]{2,1,0:T(8,128)S(1)}, bf16[2,384,192]{2,1,0:T(8,128)(2,1)S(1)}, bf16[2,2,96,192]{3,2,1,0:T(8,128)(2,1)S(1)}, bf16[2,192,192]{2,1,0:T(8,128)(2,1)S(1)}, f32[2,384]{1,0:T(2,128)S(1)}) custom-call(bf16[3,2,384,384]{3,2,1,0:T(8,128)(2,1)} %near_blocks.1, ...), custom_call_target="tpu_custom_call", output_to_operand_aliasing={{0}: (8, {}), {1}: (9, {}), {2}: (10, {}), {3}: (11, {}), {... | custom-call | tf_op jit(solution)/shard_map/pallas_call | solution.py:48
  49.9 0.0 all-to-all-done.recv
  49.9 1.6 %shard_map.70 = (f32[2,384,256]{2,1,0:T(8,128)}, f32[2,384,256]{2,1,0:T(8,128)S(1)}, bf16[2,384,384]{2,1,0:T(8,128)(2,1)S(1)}) custom-call(bf16[3,2,384,384]{3,2,1,0:T(8,128)(2,1)} %near_blocks.1, bf16[4,2,96,256]{3,2,1,0:T(8,128)(2,1)S(1)} %all-to-all-done.recv, bf16[2,2,96,192]{3,2,1,0:T(8,128)(2,1)S(1)} %get-tuple-element.45.pair, ...), custom_call_target="tpu_custom_call" | custom-call | tf_op jit(solution)/shard_map/pallas_call | solution.py:48
  51.6 1.0 %shard_map.71 = f32[2,384,256]{2,1,0:T(8,128)} custom-call(f32[2,384,256]{2,1,0:T(8,128)} %get-tuple-element.50.out_before, f32[2,384,256]{2,1,0:T(8,128)S(1)} %get-tuple-element.51.result, bf16[2,384,384]{2,1,0:T(8,128)(2,1)S(1)} %get-tuple-element.52.block, f32[2,384]{1,0:T(2,128)S(1)} %get-tuple-element.49.precondition, ...), custom_call_target="tpu_custom_call", output_to_operand_aliasing={{}: (0, {})} | custom-call | tf_op jit(solution)/shard_map/pallas_call | solution.py:48
  (4 shorter events, 0.0 us)
Async XLA Ops:
  1.7 3.8 %collective-permute-start = (bf16[2,480,256]{2,1,0:T(8,128)(2,1)S(1)}, bf16[2,480,256]{2,1,0:T(8,128)(2,1)S(1)}, u32[]{:S(2)}, u32[]{:S(2)}) collective-permute-start(bf16[2,480,256]{2,1,0:T(8,128)(2,1)S(1)} %get-tuple-element.30), channel_id=1, source_target_pairs={{0,1},{1,0},{2,3},{3,2},{4,5},{5,4},{6,7},{7,6},{8,9},{9,8},{10,11... | collective-permute-start | bytes 1474568 | tf_op jit(solution)/shard_map/ppermute | solution.py:17
  5.7 7.7 %collective-permute-start.1 = (bf16[2,96,256]{2,1,0:T(8,128)(2,1)S(1)}, bf16[2,96,256]{2,1,0:T(8,128)(2,1)S(1)}, u32[]{:S(2)}, u32[]{:S(2)}) collective-permute-start(bf16[2,96,256]{2,1,0:T(8,128)(2,1)S(1)} %get-tuple-element.33), channel_id=1, source_target_pairs={{0,2},{1,3},{2,0},{3,1},{4,6},{5,7},{6,4},{7,5},{8,10},{9,11},{10,... | collective-permute-start | bytes 294920 | tf_op jit(solution)/shard_map/ppermute | solution.py:17
  9.2 30.4 %collective-permute-start.5 = (bf16[2,384,256]{2,1,0:T(8,128)(2,1)S(1)}, bf16[2,384,256]{2,1,0:T(8,128)(2,1)S(1)}, u32[]{:S(2)}, u32[]{:S(2)}) collective-permute-start(bf16[2,384,256]{2,1,0:T(8,128)(2,1)S(1)} %get-tuple-element.38.refs_4_), channel_id=1, source_target_pairs={{511,0}} | collective-permute-start | bytes 1179656 | tf_op jit(solution)/shard_map/ppermute | solution.py:26
  9.9 36.9 %collective-permute-start.4 = (bf16[2,384,256]{2,1,0:T(8,128)(2,1)S(1)}, bf16[2,384,256]{2,1,0:T(8,128)(2,1)S(1)}, u32[]{:S(2)}, u32[]{:S(2)}) collective-permute-start(bf16[2,384,256]{2,1,0:T(8,128)(2,1)S(1)} %get-tuple-element.38.refs_4_), channel_id=1, source_target_pairs={{1,2},{2,1},{3,4},{4,3},{5,6},{6,5},{7,8},{8,7},{9,10},{10,9},{11,... | collective-permute-start | bytes 1179656 | tf_op jit(solution)/shard_map/ppermute | solution.py:22
  13.7 9.5 %collective-permute-start.2 = (bf16[2,96,256]{2,1,0:T(8,128)(2,1)S(1)}, bf16[2,96,256]{2,1,0:T(8,128)(2,1)S(1)}, u32[]{:S(2)}, u32[]{:S(2)}) collective-permute-start(bf16[2,96,256]{2,1,0:T(8,128)(2,1)S(1)} %get-tuple-element.36), channel_id=1, source_target_pairs={{0,4},{1,5},{2,6},{3,7},{4,0},{5,1},{6,2},{7,3},{8,12},{9,13},{10,... | collective-permute-start | bytes 294920 | tf_op jit(solution)/shard_map/ppermute | solution.py:17
  17.8 33.7 %collective-permute-start.6 = (bf16[2,384,256]{2,1,0:T(8,128)(2,1)S(1)}, bf16[2,384,256]{2,1,0:T(8,128)(2,1)}, u32[]{:S(2)}, u32[]{:S(2)}) collective-permute-start(bf16[2,384,256]{2,1,0:T(8,128)(2,1)S(1)} %get-tuple-element.38.refs_4_), channel_id=1, source_target_pairs={{0,511}} | collective-permute-start | bytes 1179656 | tf_op jit(solution)/shard_map/ppermute | solution.py:26
  24.2 25.7 %all-to-all-start = ((bf16[4,2,96,256]{3,2,1,0:T(8,128)(2,1)}), bf16[4,2,96,256]{3,2,1,0:T(8,128)(2,1)S(1)}, u32[]{:S(2)}, u32[]{:S(2)}) async-start(bf16[4,2,96,256]{3,2,1,0:T(8,128)(2,1)} %shard_map.67), calls=%async_computation | async-start | bytes 786432 | tf_op jit(solution)/shard_map/all_to_all | solution.py:358
  37.7 8.0 %collective-permute-start.3 = (bf16[2,96,192]{2,1,0:T(8,128)(2,1)S(1)}, bf16[2,96,192]{2,1,0:T(8,128)(2,1)S(1)}, u32[]{:S(2)}, u32[]{:S(2)}) collective-permute-start(bf16[2,96,192]{2,1,0:T(8,128)(2,1)S(1)} %get-tuple-element.39), channel_id=1, source_target_pairs={{0,16},{1,17},{2,18},{3,19},{4,20},{5,21},{6,22},{7,23},{8,24},{9,... | collective-permute-start | bytes 221192 | tf_op jit(solution)/shard_map/ppermute | solution.py:17
  39.6 0.8 %copy-start = (bf16[2,384,256]{2,1,0:T(8,128)(2,1)}, bf16[2,384,256]{2,1,0:T(8,128)(2,1)S(1)}, u32[]{:S(2)}) copy-start(bf16[2,384,256]{2,1,0:T(8,128)(2,1)S(1)} %collective-permute-done.5.refs_7_) | copy-start | bytes 1179652
  45.7 1.0 %copy-start.1 = (bf16[2,384,256]{2,1,0:T(8,128)(2,1)S(1)}, bf16[2,384,256]{2,1,0:T(8,128)(2,1)}, u32[]{:S(2)}) copy-start(bf16[2,384,256]{2,1,0:T(8,128)(2,1)} %copy-done) | copy-start | bytes 1179652

commit v5 on v4

--- a/solution.py
+++ b/solution.py
@@ -239,14 +239,13 @@
     return lax.axis_index("seg") == lax.axis_size("seg") - 1
 
 
-def finish_kernel(out_before, result, block, precondition, from_first, out, buf, sems):
+def finish_kernel(out_before, result, block, columns, from_first, out, buf, sems):
     @pl.when(at_final())
     def _():
-        pre = jnp.transpose(precondition[...])
         copies = []
         for part, span in enumerate(parts_of(result.shape[1])):
             real, imag = product(block[0, span], block[1, span], from_first[0], from_first[1])
-            real, imag = weighted(pre[span], real, imag)
+            real, imag = weighted(columns[span], real, imag)
             buf[0, span] = result[0, span] + real
             buf[1, span] = result[1, span] + imag
             copy = pltpu.make_async_copy(buf.at[:, span], out.at[:, span], sems.at[part])
@@ -272,6 +271,7 @@
     out,
     result,
     block,
+    columns,
     joined,
     sems,
 ):
@@ -290,6 +290,7 @@
         copy = pltpu.make_async_copy(result.at[:, span], out.at[:, span], sems.at[part])
         copy.start()
         copies.append(copy)
+    columns[...] = pre
     for copy in copies:
         copy.wait()
     pl.when(at_final())(fetch.wait)
@@ -385,20 +386,20 @@
         )
     near, turned, pair, matrix4, scales = done
     out = jax.ShapeDtypeStruct((2, rows, angles), F32)
-    out, result, last_block = call(
+    out, result, last_block, columns = call(
         last_kernel,
         6,
-        (out, whole, pltpu.VMEM(near_blocks.shape[1:], BF16)),
+        (out, whole, pltpu.VMEM(near_blocks.shape[1:], BF16), pltpu.VMEM((rows, 2), F32)),
         (near_blocks, recv, pair, matrix4, turned, near, scales),
         in_specs=[HBM] + [VMEM] * 6,
-        out_specs=[HBM, VMEM, VMEM],
+        out_specs=[HBM, VMEM, VMEM, VMEM],
         scratch=[joined, pltpu.SemaphoreType.DMA((4,))],
     )
     return call(
         finish_kernel,
         4,
         jax.ShapeDtypeStruct((2, rows, angles), F32),
-        (out, result, last_block, scales, from_first),
+        (out, result, last_block, columns, from_first),
         in_specs=[HBM] + [VMEM] * 4,
         out_specs=HBM,
         scratch=[pltpu.VMEM((2, rows, angles), F32), pltpu.SemaphoreType.DMA((3,))],

time: 53 us -> 51.3 us (0.968)
  starting transfers between devices: 30.5 us -> 29.1 us
  Pallas kernels: 9.07 us -> 8.07 us
  waiting for transfers between devices: 11.1 us -> 11.8 us
    pallas_call x8, Pallas kernels: 9.07 us -> 8.07 us  [call(): pl.pallas_call(kernel, out_shape=out_shape, in_specs=in_specs, out_specs=...]
    ppermute x2, starting transfers between devices: 2.11 us -> 1.37 us  [moved(): return lax.ppermute(array, 'seg', [(source, target)])]
    ppermute x4, waiting for transfers between devices: 11.1 us -> 11.8 us  [swapped(): lax.ppermute(array, 'seg', [(i, i ^ mask) for i in range(lax.axis_size('s...]
    all_to_all x1, starting transfers between devices: 13.5 us -> 12.7 us  [body(): lax.all_to_all(send, 'seg', 0, 0, axis_index_groups=groups_of_four(3))]
where the time goes in v5:
time: 51.3 us; the launch traced here: 50.9 us
  starting transfers between devices  29.1 us (57%)
  waiting for transfers between devices  11.8 us (23%)
  Pallas kernels  8.07 us (16%)
  local copies, waits for them, and re-layouts  1.74 us (3%)
    all_to_all x1, starting transfers between devices, body(): lax.all_to_all(send, 'seg', 0, 0, axis_index_groups=groups_of_four(3))  12.7 us
    ppermute x4, waiting for transfers between devices, swapped(): lax.ppermute(array, 'seg', [(i, i ^ mask) for i in range(lax.axis_size('s...  11.8 us
    ppermute x4, starting transfers between devices, swapped(): lax.ppermute(array, 'seg', [(i, i ^ mask) for i in range(lax.axis_size('s...  11.4 us
    pallas_call x8, Pallas kernels, call(): pl.pallas_call(kernel, out_shape=out_shape, in_specs=in_specs, out_specs=...  8.07 us
    ppermute x1, starting transfers between devices, swapped_across(): lax.ppermute(array, 'seg', [(i, (i + 1 ^ 1) - 1) for i in range(1, size -...  3.52 us
    unnamed x4, local copies, waits for them, and re-layouts  1.74 us
    ppermute x2, starting transfers between devices, moved(): return lax.ppermute(array, 'seg', [(source, target)])  1.37 us
  transfers between devices with their start and end apart: 8, of which 3 were waited for; matrix products, arithmetic and copies ran while one was open for 0% of the time, Pallas kernels for 12%

profile of v5, /device:TPU:2, one launch (start us, length us, event | category | flops | bytes accessed | tf_op | source)
XLA Modules:
  0.0 50.9 jit_solution(13827407642031562961)
XLA Ops:
  0.0 1.6 %shard_map.64 = (bf16[2,384,256]{2,1,0:T(8,128)(2,1)S(1)}, bf16[2,96,256]{2,1,0:T(8,128)(2,1)S(1)}, bf16[2,480,256]{2,1,0:T(8,128)(2,1)S(1)}, bf16[2,288,192]{2,...) custom-call(f32[2,384,256]{2,1,0:T(8,128)} %density.1, ...), custom_call_target="tpu_custom_call" | custom-call | tf_op jit(solution)/shard_map/pallas_call | solution.py:48
  1.7 1.9 %collective-permute-start = (bf16[2,480,256]{2,1,0:T(8,128)(2,1)S(1)}, bf16[2,480,256]{2,1,0:T(8,128)(2,1)S(1)}, u32[]{:S(2)}, u32[]{:S(2)}) collective-permute-start(bf16[2,480,256]{2,1,0:T(8,128)(2,1)S(1)} %get-tuple-element.31), channel_id=1, source_target_pairs={{0,1},{1,0},{2,3},{3,2},{4,5},{5,4},{6,7},{7,6},{8,9},{9,8},{10,11... | collective-permute-start | bytes 1474568 | tf_op jit(solution)/shard_map/ppermute | solution.py:17
  3.6 1.8 %collective-permute-done.recv.refs_5_ = bf16[2,480,256]{2,1,0:T(8,128)(2,1)S(1)} collective-permute-done((bf16[2,480,256]{2,1,0:T(8,128)(2,1)S(1)}, bf16[2,480,256]{2,1,0:T(8,128)(2,1)S(1)}, u32[]{:S(2)}, u32[]{:S(2)}) %collective-permute-start) | collective-permute-done | bytes 491552 | tf_op jit(solution)/shard_map/ppermute | solution.py:17
  5.4 0.3 shard_map.65
  5.7 3.5 %collective-permute-start.1 = (bf16[2,96,256]{2,1,0:T(8,128)(2,1)S(1)}, bf16[2,96,256]{2,1,0:T(8,128)(2,1)S(1)}, u32[]{:S(2)}, u32[]{:S(2)}) collective-permute-start(bf16[2,96,256]{2,1,0:T(8,128)(2,1)S(1)} %get-tuple-element.34), channel_id=1, source_target_pairs={{0,2},{1,3},{2,0},{3,1},{4,6},{5,7},{6,4},{7,5},{8,10},{9,11},{10,... | collective-permute-start | bytes 294920 | tf_op jit(solution)/shard_map/ppermute | solution.py:17
  9.2 0.7 %collective-permute-start.5 = (bf16[2,384,256]{2,1,0:T(8,128)(2,1)S(1)}, bf16[2,384,256]{2,1,0:T(8,128)(2,1)S(1)}, u32[]{:S(2)}, u32[]{:S(2)}) collective-permute-start(bf16[2,384,256]{2,1,0:T(8,128)(2,1)S(1)} %get-tuple-element.39.refs_4_), channel_id=1, source_target_pairs={{511,0}} | collective-permute-start | bytes 1179656 | tf_op jit(solution)/shard_map/ppermute | solution.py:26
  9.9 3.5 %collective-permute-start.4 = (bf16[2,384,256]{2,1,0:T(8,128)(2,1)S(1)}, bf16[2,384,256]{2,1,0:T(8,128)(2,1)}, u32[]{:S(2)}, u32[]{:S(2)}) collective-permute-start(bf16[2,384,256]{2,1,0:T(8,128)(2,1)S(1)} %get-tuple-element.39.refs_4_), channel_id=1, source_target_pairs={{1,2},{2,1},{3,4},{4,3},{5,6},{6,5},{7,8},{8,7},{9,10},{10,9},{11,... | collective-permute-start | bytes 1179656 | tf_op jit(solution)/shard_map/ppermute | solution.py:22
  13.4 0.0 collective-permute-done.1.refs_1_
  13.4 0.3 shard_map.66
  13.7 4.1 %collective-permute-start.2 = (bf16[2,96,256]{2,1,0:T(8,128)(2,1)S(1)}, bf16[2,96,256]{2,1,0:T(8,128)(2,1)S(1)}, u32[]{:S(2)}, u32[]{:S(2)}) collective-permute-start(bf16[2,96,256]{2,1,0:T(8,128)(2,1)S(1)} %get-tuple-element.37), channel_id=1, source_target_pairs={{0,4},{1,5},{2,6},{3,7},{4,0},{5,1},{6,2},{7,3},{8,12},{9,13},{10,... | collective-permute-start | bytes 294920 | tf_op jit(solution)/shard_map/ppermute | solution.py:17
  17.8 0.7 %collective-permute-start.6 = (bf16[2,384,256]{2,1,0:T(8,128)(2,1)S(1)}, bf16[2,384,256]{2,1,0:T(8,128)(2,1)S(1)}, u32[]{:S(2)}, u32[]{:S(2)}) collective-permute-start(bf16[2,384,256]{2,1,0:T(8,128)(2,1)S(1)} %get-tuple-element.39.refs_4_), channel_id=1, source_target_pairs={{0,511}} | collective-permute-start | bytes 1179656 | tf_op jit(solution)/shard_map/ppermute | solution.py:26
  18.5 4.7 %collective-permute-done.2.refs_1_ = bf16[2,96,256]{2,1,0:T(8,128)(2,1)S(1)} collective-permute-done((bf16[2,96,256]{2,1,0:T(8,128)(2,1)S(1)}, bf16[2,96,256]{2,1,0:T(8,128)(2,1)S(1)}, u32[]{:S(2)}, u32[]{:S(2)}) %collective-permute-start.2) | collective-permute-done | bytes 98336 | tf_op jit(solution)/shard_map/ppermute | solution.py:17
  23.2 1.0 %shard_map.67 = bf16[4,2,96,256]{3,2,1,0:T(8,128)(2,1)} custom-call(bf16[2,96,256]{2,1,0:T(8,128)(2,1)S(1)} %get-tuple-element.36.refs_0_, bf16[2,96,256]{2,1,0:T(8,128)(2,1)S(1)} %collective-permute-done.2.refs_1_, bf16[2,192,192]{2,1,0:T(8,128)(2,1)S(1)} %get-tuple-element.38.refs_2_), custom_call_target="tpu_custom_call" | custom-call | tf_op jit(solution)/shard_map/pallas_call | solution.py:48
  24.2 12.7 %all-to-all-start = ((bf16[4,2,96,256]{3,2,1,0:T(8,128)(2,1)}), bf16[4,2,96,256]{3,2,1,0:T(8,128)(2,1)S(1)}, u32[]{:S(2)}, u32[]{:S(2)}) async-start(bf16[4,2,96,256]{3,2,1,0:T(8,128)(2,1)} %shard_map.67), calls=%async_computation | async-start | bytes 786432 | tf_op jit(solution)/shard_map/all_to_all | solution.py:359
  37.0 1.9 %collective-permute-start.3 = (bf16[2,96,192]{2,1,0:T(8,128)(2,1)S(1)}, bf16[2,96,192]{2,1,0:T(8,128)(2,1)S(1)}, u32[]{:S(2)}, u32[]{:S(2)}) collective-permute-start(bf16[2,96,192]{2,1,0:T(8,128)(2,1)S(1)} %get-tuple-element.40), channel_id=1, source_target_pairs={{0,16},{1,17},{2,18},{3,19},{4,20},{5,21},{6,22},{7,23},{8,24},{9,... | collective-permute-start | bytes 221192 | tf_op jit(solution)/shard_map/ppermute | solution.py:17
  38.9 0.0 collective-permute-done.5.refs_7_
  38.9 0.7 %copy-done = bf16[2,384,256]{2,1,0:T(8,128)(2,1)} copy-done((bf16[2,384,256]{2,1,0:T(8,128)(2,1)}, bf16[2,384,256]{2,1,0:T(8,128)(2,1)S(1)}, u32[]{:S(2)}) %copy-start) | copy-done | bytes 393240
  39.6 5.3 %collective-permute-done.3.refs_6_ = bf16[2,96,192]{2,1,0:T(8,128)(2,1)S(1)} collective-permute-done((bf16[2,96,192]{2,1,0:T(8,128)(2,1)S(1)}, bf16[2,96,192]{2,1,0:T(8,128)(2,1)S(1)}, u32[]{:S(2)}, u32[]{:S(2)}) %collective-permute-start.3) | collective-permute-done | bytes 73760 | tf_op jit(solution)/shard_map/ppermute | solution.py:17
  45.0 1.0 %copy-done.1 = bf16[2,384,256]{2,1,0:T(8,128)(2,1)S(1)} copy-done((bf16[2,384,256]{2,1,0:T(8,128)(2,1)S(1)}, bf16[2,384,256]{2,1,0:T(8,128)(2,1)}, u32[]{:S(2)}) %copy-start.1) | copy-done | bytes 393240
  46.0 0.1 shard_map.68
  46.1 0.0 collective-permute-done.4.refs_7_
  46.1 3.1 %shard_map.69 = (f32[2,384,256]{2,1,0:T(8,128)S(1)}, bf16[2,384,192]{2,1,0:T(8,128)(2,1)S(1)}, bf16[2,2,96,192]{3,2,1,0:T(8,128)(2,1)S(1)}, bf16[2,192,192]{2,1,0:T(8,128)(2,1)S(1)}, f32[2,384]{1,0:T(2,128)S(1)}) custom-call(bf16[3,2,384,384]{3,2,1,0:T(8,128)(2,1)} %near_blocks.1, ...), custom_call_target="tpu_custom_call", output_to_operand_aliasing={{0}: (8, {}), {1}: (9, {}), {2}: (10, {}), {3}: (11, {}), {... | custom-call | tf_op jit(solution)/shard_map/pallas_call | solution.py:48
  49.2 0.0 all-to-all-done.recv
  49.2 1.6 %shard_map.70 = (f32[2,384,256]{2,1,0:T(8,128)}, f32[2,384,256]{2,1,0:T(8,128)S(1)}, bf16[2,384,384]{2,1,0:T(8,128)(2,1)S(1)}, f32[384,2]{1,0:T(8,128)S(1)}) custom-call(bf16[3,2,384,384]{3,2,1,0:T(8,128)(2,1)} %near_blocks.1, bf16[4,2,96,256]{3,2,1,0:T(8,128)(2,1)S(1)} %all-to-all-done.recv, bf16[2,2,96,192]{3,2,1,0:T(8,128)(2,1)S(1)} %get-tuple-element.46.pair, ...), custom_call_target="tpu_custom_call" | custom-call | tf_op jit(solution)/shard_map/pallas_call | solution.py:48
  (4 shorter events, 0.1 us)
Async XLA Ops:
  1.7 3.8 %collective-permute-start = (bf16[2,480,256]{2,1,0:T(8,128)(2,1)S(1)}, bf16[2,480,256]{2,1,0:T(8,128)(2,1)S(1)}, u32[]{:S(2)}, u32[]{:S(2)}) collective-permute-start(bf16[2,480,256]{2,1,0:T(8,128)(2,1)S(1)} %get-tuple-element.31), channel_id=1, source_target_pairs={{0,1},{1,0},{2,3},{3,2},{4,5},{5,4},{6,7},{7,6},{8,9},{9,8},{10,11... | collective-permute-start | bytes 1474568 | tf_op jit(solution)/shard_map/ppermute | solution.py:17
  5.7 7.7 %collective-permute-start.1 = (bf16[2,96,256]{2,1,0:T(8,128)(2,1)S(1)}, bf16[2,96,256]{2,1,0:T(8,128)(2,1)S(1)}, u32[]{:S(2)}, u32[]{:S(2)}) collective-permute-start(bf16[2,96,256]{2,1,0:T(8,128)(2,1)S(1)} %get-tuple-element.34), channel_id=1, source_target_pairs={{0,2},{1,3},{2,0},{3,1},{4,6},{5,7},{6,4},{7,5},{8,10},{9,11},{10,... | collective-permute-start | bytes 294920 | tf_op jit(solution)/shard_map/ppermute | solution.py:17
  9.2 29.7 %collective-permute-start.5 = (bf16[2,384,256]{2,1,0:T(8,128)(2,1)S(1)}, bf16[2,384,256]{2,1,0:T(8,128)(2,1)S(1)}, u32[]{:S(2)}, u32[]{:S(2)}) collective-permute-start(bf16[2,384,256]{2,1,0:T(8,128)(2,1)S(1)} %get-tuple-element.39.refs_4_), channel_id=1, source_target_pairs={{511,0}} | collective-permute-start | bytes 1179656 | tf_op jit(solution)/shard_map/ppermute | solution.py:26
  9.9 36.2 %collective-permute-start.4 = (bf16[2,384,256]{2,1,0:T(8,128)(2,1)S(1)}, bf16[2,384,256]{2,1,0:T(8,128)(2,1)}, u32[]{:S(2)}, u32[]{:S(2)}) collective-permute-start(bf16[2,384,256]{2,1,0:T(8,128)(2,1)S(1)} %get-tuple-element.39.refs_4_), channel_id=1, source_target_pairs={{1,2},{2,1},{3,4},{4,3},{5,6},{6,5},{7,8},{8,7},{9,10},{10,9},{11,... | collective-permute-start | bytes 1179656 | tf_op jit(solution)/shard_map/ppermute | solution.py:22
  13.7 9.5 %collective-permute-start.2 = (bf16[2,96,256]{2,1,0:T(8,128)(2,1)S(1)}, bf16[2,96,256]{2,1,0:T(8,128)(2,1)S(1)}, u32[]{:S(2)}, u32[]{:S(2)}) collective-permute-start(bf16[2,96,256]{2,1,0:T(8,128)(2,1)S(1)} %get-tuple-element.37), channel_id=1, source_target_pairs={{0,4},{1,5},{2,6},{3,7},{4,0},{5,1},{6,2},{7,3},{8,12},{9,13},{10,... | collective-permute-start | bytes 294920 | tf_op jit(solution)/shard_map/ppermute | solution.py:17
  17.8 33.0 %collective-permute-start.6 = (bf16[2,384,256]{2,1,0:T(8,128)(2,1)S(1)}, bf16[2,384,256]{2,1,0:T(8,128)(2,1)S(1)}, u32[]{:S(2)}, u32[]{:S(2)}) collective-permute-start(bf16[2,384,256]{2,1,0:T(8,128)(2,1)S(1)} %get-tuple-element.39.refs_4_), channel_id=1, source_target_pairs={{0,511}} | collective-permute-start | bytes 1179656 | tf_op jit(solution)/shard_map/ppermute | solution.py:26
  24.2 25.0 %all-to-all-start = ((bf16[4,2,96,256]{3,2,1,0:T(8,128)(2,1)}), bf16[4,2,96,256]{3,2,1,0:T(8,128)(2,1)S(1)}, u32[]{:S(2)}, u32[]{:S(2)}) async-start(bf16[4,2,96,256]{3,2,1,0:T(8,128)(2,1)} %shard_map.67), calls=%async_computation | async-start | bytes 786432 | tf_op jit(solution)/shard_map/all_to_all | solution.py:359
  37.0 8.0 %collective-permute-start.3 = (bf16[2,96,192]{2,1,0:T(8,128)(2,1)S(1)}, bf16[2,96,192]{2,1,0:T(8,128)(2,1)S(1)}, u32[]{:S(2)}, u32[]{:S(2)}) collective-permute-start(bf16[2,96,192]{2,1,0:T(8,128)(2,1)S(1)} %get-tuple-element.40), channel_id=1, source_target_pairs={{0,16},{1,17},{2,18},{3,19},{4,20},{5,21},{6,22},{7,23},{8,24},{9,... | collective-permute-start | bytes 221192 | tf_op jit(solution)/shard_map/ppermute | solution.py:17
  38.9 0.8 %copy-start = (bf16[2,384,256]{2,1,0:T(8,128)(2,1)}, bf16[2,384,256]{2,1,0:T(8,128)(2,1)S(1)}, u32[]{:S(2)}) copy-start(bf16[2,384,256]{2,1,0:T(8,128)(2,1)S(1)} %collective-permute-done.5.refs_7_) | copy-start | bytes 1179652
  45.0 1.0 %copy-start.1 = (bf16[2,384,256]{2,1,0:T(8,128)(2,1)S(1)}, bf16[2,384,256]{2,1,0:T(8,128)(2,1)}, u32[]{:S(2)}) copy-start(bf16[2,384,256]{2,1,0:T(8,128)(2,1)} %copy-done) | copy-start | bytes 1179652
